TPU v7x, 32 devices: a whole 2x2x4 slice. The times are simulated.
32 devices in a mesh: ctx: 8 (over y, x, core), fsdp: 4 (over z).
Axes of the slice: x: 2, y: 2, z: 4, core: 2. Of those that a mesh axis runs over, the one named last changes fastest.
Arguments:
- hidden: bfloat16 [4096, 1536], P(('fsdp', 'ctx')), may hold values from -6 to 6
- positions: int32 [4096], P('fsdp'), may hold values from 0 to 1023, as said below
- first_gain: bfloat16 [1536], P(('ctx', 'fsdp')), may hold values from 0.099609375 to 1.8984375
- query_weight: bfloat16 [1536, 1536], P(('ctx', 'fsdp')), may hold values from -0.15625 to 0.15625
- key_weight: bfloat16 [1536, 256], P(('ctx', 'fsdp')), may hold values from -0.15625 to 0.15625
- value_weight: bfloat16 [1536, 256], P(('ctx', 'fsdp')), may hold values from -0.15625 to 0.15625
- query_bias: bfloat16 [1536], P(('ctx', 'fsdp')), may hold values from -3 to 3
- key_bias: bfloat16 [256], P(('ctx', 'fsdp')), may hold values from -3 to 3
- value_bias: bfloat16 [256], P(('ctx', 'fsdp')), may hold values from -3 to 3
- output_weight: bfloat16 [1536, 1536], P(('ctx', 'fsdp')), may hold values from -0.625 to 0.625
- second_gain: bfloat16 [1536], P(('ctx', 'fsdp')), may hold values from 0.099609375 to 1.8984375
- gate_weight: bfloat16 [1536, 8960], P(None, ('ctx', 'fsdp')), may hold values from -0.15625 to 0.15625
- up_weight: bfloat16 [1536, 8960], P(None, ('ctx', 'fsdp')), may hold values from -0.15625 to 0.15625
- down_weight: bfloat16 [8960, 1536], P(('ctx', 'fsdp')), may hold values from -0.0625 to 0.0625
- cotangent: bfloat16 [4096, 1536], P(('fsdp', 'ctx')), may hold values from -6 to 6
Outputs:
- layer_output: bfloat16 [4096, 1536], P(('fsdp', 'ctx'))
- input_gradient: float32 [4096, 1536], P(('fsdp', 'ctx'))
- first_gain_gradient: float32 [1536], P(('ctx', 'fsdp'))
- query_weight_gradient: float32 [1536, 1536], P(('ctx', 'fsdp'))
- key_weight_gradient: float32 [1536, 256], P(('ctx', 'fsdp'))
- value_weight_gradient: float32 [1536, 256], P(('ctx', 'fsdp'))
- query_bias_gradient: float32 [1536], P(('ctx', 'fsdp'))
- key_bias_gradient: float32 [256], P(('ctx', 'fsdp'))
- value_bias_gradient: float32 [256], P(('ctx', 'fsdp'))
- output_weight_gradient: float32 [1536, 1536], P(('ctx', 'fsdp'))
- second_gain_gradient: float32 [1536], P(('ctx', 'fsdp'))
- gate_weight_gradient: float32 [1536, 8960], P(None, ('ctx', 'fsdp'))
- up_weight_gradient: float32 [1536, 8960], P(None, ('ctx', 'fsdp'))
- down_weight_gradient: float32 [8960, 1536], P(('ctx', 'fsdp'))
Inputs may be any that keep to these rules, and one draw needn't show every extreme that they name: Within each sequence of 1024 tokens, the 128 tokens of each index of ctx are two runs of consecutive positions of 64 each: blocks b and 15 - b of the sequence cut into 16 equal blocks, the earlier block first, where b (0 to 7) may differ for each index of ctx and each sequence; every position of the sequence appears once.
All inputs are finite; a program needn't handle non-finite values.
Results may differ from a plain program's by a relative error of at most 0.035.
Values may be sent and summed in bfloat16 or wider, within the bound.
No kernel may reach another device: no remote copies, remote signals or barrier semaphores. Data moves between devices by JAX's collectives and lax.ppermute only.
A program may use at most 256 MiB of HBM per device.

v0:
```python
import jax
import jax.numpy as jnp
from jax import lax
from jax.sharding import PartitionSpec as P

H = 12
KV = 2
HD = 128


epsilon = 1e-06
rope_base = 1000000.0
neg_large = -1e30


def rms_norm(values, norm_gain):
    return (
        values * lax.rsqrt(jnp.mean(values * values, axis=-1, keepdims=True) + epsilon) * norm_gain
    )


def rotate(values, places):
    half_width = values.shape[-1] // 2
    frequency = rope_base ** (-2.0 * jnp.arange(half_width, dtype=jnp.float32) / values.shape[-1])
    angles = places.astype(jnp.float32)[:, None] * frequency[None, :]
    cosine = jnp.cos(angles)[:, None, :]
    sine_table = jnp.sin(angles)[:, None, :]
    leading = values[..., :half_width]
    trailing = values[..., half_width:]
    return jnp.concatenate(
        [leading * cosine - trailing * sine_table, trailing * cosine + leading * sine_table],
        axis=-1,
    )


def matmul(left, right):
    return jnp.dot(left, right, preferred_element_type=jnp.float32)


def inner(left, right):
    return lax.dot_general(
        left, right, (((0,), (0,)), ((), ())), preferred_element_type=jnp.float32
    )


def gated(gate_in, up_in):
    return jax.nn.silu(gate_in) * up_in


def local(
    hidden,
    positions,
    first_gain,
    query_weight,
    key_weight,
    value_weight,
    query_bias,
    key_bias,
    value_bias,
    output_weight,
    second_gain,
    gate_weight,
    up_weight,
    down_weight,
    cotangent,
):
    rows_here = hidden.shape[0]
    sequence_len = positions.shape[0]
    group_size = H // KV
    score_scale = HD ** (-0.5)
    ctx_count = lax.axis_size("ctx")
    ctx_here = lax.axis_index("ctx")
    own_places = lax.dynamic_slice_in_dim(positions, ctx_here * rows_here, rows_here)
    (
        gain_one,
        weight_query,
        weight_key,
        weight_value,
        bias_query,
        bias_key,
        bias_value,
        weight_output,
        gain_two,
    ) = (
        lax.all_gather(first_gain, ("ctx", "fsdp"), axis=0, tiled=True),
        lax.all_gather(query_weight, ("ctx", "fsdp"), axis=0, tiled=True),
        lax.all_gather(key_weight, ("ctx", "fsdp"), axis=0, tiled=True),
        lax.all_gather(value_weight, ("ctx", "fsdp"), axis=0, tiled=True),
        lax.all_gather(query_bias, ("ctx", "fsdp"), axis=0, tiled=True),
        lax.all_gather(key_bias, ("ctx", "fsdp"), axis=0, tiled=True),
        lax.all_gather(value_bias, ("ctx", "fsdp"), axis=0, tiled=True),
        lax.all_gather(output_weight, ("ctx", "fsdp"), axis=0, tiled=True),
        lax.all_gather(second_gain, ("ctx", "fsdp"), axis=0, tiled=True),
    )
    inputs = hidden.astype(jnp.float32)
    normed = rms_norm(inputs, gain_one.astype(jnp.float32)).astype(jnp.bfloat16)
    query_lin = matmul(normed, weight_query) + bias_query.astype(jnp.float32)
    key_lin = matmul(normed, weight_key) + bias_key.astype(jnp.float32)
    value_lin = matmul(normed, weight_value) + bias_value.astype(jnp.float32)
    queries = (
        rotate(query_lin.reshape(rows_here, H, HD), own_places)
        .astype(jnp.bfloat16)
        .reshape(rows_here, KV, group_size, HD)
    )
    keys_local = (
        rotate(key_lin.reshape(rows_here, KV, HD), own_places)
        .astype(jnp.bfloat16)
        .reshape(rows_here, KV * HD)
    )
    values_local = value_lin.astype(jnp.bfloat16)
    keys_all, values_all = (
        lax.all_gather(keys_local, "ctx", axis=0, tiled=True),
        lax.all_gather(values_local, "ctx", axis=0, tiled=True),
    )
    block_rows = min(512, sequence_len)
    block_count = sequence_len // block_rows
    key_blocks = keys_all.reshape(block_count, block_rows, KV, HD)
    value_blocks = values_all.reshape(block_count, block_rows, KV, HD)
    place_blocks = positions.reshape(block_count, block_rows)

    def masked_scores(key_block, place_block):
        scores = (
            jnp.einsum("tgjd,sgd->gjts", queries, key_block, preferred_element_type=jnp.float32)
            * score_scale
        )
        allowed = place_block[None, None, None, :] <= own_places[None, None, :, None]
        return (scores, allowed)

    def top_step(state_pair, pieces):
        running_top, running_total = state_pair
        scores, allowed = masked_scores(pieces[0], pieces[1])
        scores = jnp.where(allowed, scores, neg_large)
        new_top = jnp.maximum(running_top, jnp.max(scores, axis=-1))
        exp_terms = jnp.where(allowed, jnp.exp(scores - new_top[..., None]), 0.0)
        running_total = running_total * jnp.exp(running_top - new_top) + jnp.sum(exp_terms, axis=-1)
        return ((new_top, running_total), None)

    start_top = jnp.full((KV, group_size, rows_here), neg_large, jnp.float32)
    start_total = jnp.zeros((KV, group_size, rows_here), jnp.float32)
    (top_final, total_final), unused = lax.scan(
        top_step, (start_top, start_total), (key_blocks, place_blocks)
    )
    log_sum = top_final + jnp.log(total_final)

    def weights_of(key_block, place_block):
        scores, allowed = masked_scores(key_block, place_block)
        return jnp.where(allowed, jnp.exp(scores - log_sum[..., None]), 0.0)

    def mix_step(accum, pieces):
        probs = weights_of(pieces[0], pieces[2]).astype(jnp.bfloat16)
        return (
            accum
            + jnp.einsum("gjts,sgd->tgjd", probs, pieces[1], preferred_element_type=jnp.float32),
            None,
        )

    mix_start = jnp.zeros((rows_here, KV, group_size, HD), jnp.float32)
    mixture, unused = lax.scan(mix_step, mix_start, (key_blocks, value_blocks, place_blocks))
    mixed_low = mixture.reshape(rows_here, H * HD).astype(jnp.bfloat16)
    middle = inputs + matmul(mixed_low, weight_output)
    normed_two = rms_norm(middle, gain_two.astype(jnp.float32)).astype(jnp.bfloat16)
    weight_gate, weight_up, weight_down = (
        lax.all_gather(gate_weight, ("ctx", "fsdp"), axis=1, tiled=True),
        lax.all_gather(up_weight, ("ctx", "fsdp"), axis=1, tiled=True),
        lax.all_gather(down_weight, ("ctx", "fsdp"), axis=0, tiled=True),
    )
    gate_lin = matmul(normed_two, weight_gate)
    up_lin = matmul(normed_two, weight_up)
    activated = gated(gate_lin, up_lin).astype(jnp.bfloat16)
    layer_out = (middle + matmul(activated, weight_down)).astype(jnp.bfloat16)
    activated_delta = matmul(cotangent, weight_down.T).astype(jnp.bfloat16)
    unused, gated_pull = jax.vjp(gated, gate_lin, up_lin)
    gate_delta, up_delta = gated_pull(activated_delta.astype(jnp.float32))
    gate_low = gate_delta.astype(jnp.bfloat16)
    up_low = up_delta.astype(jnp.bfloat16)
    normed_two_delta = matmul(gate_low, weight_gate.T) + matmul(up_low, weight_up.T)
    gate_cols, up_cols, active_cols = (
        lax.all_to_all(gate_low, "ctx", split_axis=1, concat_axis=0, tiled=True),
        lax.all_to_all(up_low, "ctx", split_axis=1, concat_axis=0, tiled=True),
        lax.all_to_all(activated, "ctx", split_axis=1, concat_axis=0, tiled=True),
    )
    normed_seq, cotangent_seq = (
        lax.all_gather(normed_two, "ctx", axis=0, tiled=True),
        lax.all_gather(cotangent, "ctx", axis=0, tiled=True),
    )
    gate_weight_delta, up_weight_delta, down_weight_delta = (
        lax.psum_scatter(
            inner(normed_seq, gate_cols).astype(jnp.bfloat16),
            "fsdp",
            scatter_dimension=1,
            tiled=True,
        ).astype(jnp.float32),
        lax.psum_scatter(
            inner(normed_seq, up_cols).astype(jnp.bfloat16), "fsdp", scatter_dimension=1, tiled=True
        ).astype(jnp.float32),
        lax.psum_scatter(
            inner(active_cols, cotangent_seq).astype(jnp.bfloat16),
            "fsdp",
            scatter_dimension=0,
            tiled=True,
        ).astype(jnp.float32),
    )
    unused, second_pull = jax.vjp(rms_norm, middle, gain_two.astype(jnp.float32))
    middle_part, second_gain_delta = second_pull(normed_two_delta)
    middle_delta = cotangent.astype(jnp.float32) + middle_part
    attention_low = middle_delta.astype(jnp.bfloat16)
    mixed_delta = (
        matmul(attention_low, weight_output.T)
        .astype(jnp.bfloat16)
        .reshape(rows_here, KV, group_size, HD)
    )
    row_dots = jnp.transpose(jnp.sum(mixed_delta.astype(jnp.float32) * mixture, axis=-1), (1, 2, 0))

    def back_step(query_accum, pieces):
        key_block, value_block, place_block = pieces
        probs = weights_of(key_block, place_block)
        value_part = jnp.einsum(
            "gjts,tgjd->sgd",
            probs.astype(jnp.bfloat16),
            mixed_delta,
            preferred_element_type=jnp.float32,
        )
        prob_delta = jnp.einsum(
            "tgjd,sgd->gjts", mixed_delta, value_block, preferred_element_type=jnp.float32
        )
        score_delta = (probs * (prob_delta - row_dots[..., None])).astype(jnp.bfloat16)
        query_accum = query_accum + jnp.einsum(
            "gjts,sgd->tgjd", score_delta, key_block, preferred_element_type=jnp.float32
        )
        key_part = jnp.einsum(
            "gjts,tgjd->sgd", score_delta, queries, preferred_element_type=jnp.float32
        )
        return (query_accum, (key_part, value_part))

    query_accum, (key_parts, value_parts) = lax.scan(
        back_step, mix_start, (key_blocks, value_blocks, place_blocks)
    )
    keys_delta_all = key_parts.reshape(sequence_len, KV * HD) * score_scale
    values_delta_all = value_parts.reshape(sequence_len, KV * HD)
    keys_delta, values_delta = (
        lax.psum_scatter(
            keys_delta_all.astype(jnp.bfloat16), "ctx", scatter_dimension=0, tiled=True
        ).astype(jnp.float32),
        lax.psum_scatter(
            values_delta_all.astype(jnp.bfloat16), "ctx", scatter_dimension=0, tiled=True
        ).astype(jnp.float32),
    )

    def rotate_here(values):
        return rotate(values, own_places)

    unused, key_rot_pull = jax.vjp(rotate_here, key_lin.reshape(rows_here, KV, HD))
    key_lin_delta = (
        key_rot_pull(keys_delta.reshape(rows_here, KV, HD))[0]
        .reshape(rows_here, KV * HD)
        .astype(jnp.bfloat16)
    )
    unused, query_rot_pull = jax.vjp(rotate_here, query_lin.reshape(rows_here, H, HD))
    query_lin_delta = (
        query_rot_pull((query_accum * score_scale).reshape(rows_here, H, HD))[0]
        .reshape(rows_here, H * HD)
        .astype(jnp.bfloat16)
    )
    value_lin_delta = values_delta.astype(jnp.bfloat16)
    normed_delta = (
        matmul(query_lin_delta, weight_query.T)
        + matmul(key_lin_delta, weight_key.T)
        + matmul(value_lin_delta, weight_value.T)
    )
    unused, first_pull = jax.vjp(rms_norm, inputs, gain_one.astype(jnp.float32))
    input_part, first_gain_delta = first_pull(normed_delta)
    input_delta = middle_delta + input_part
    normed_cols, mixed_cols = (
        lax.all_to_all(normed, "ctx", split_axis=1, concat_axis=0, tiled=True),
        lax.all_to_all(mixed_low, "ctx", split_axis=1, concat_axis=0, tiled=True),
    )
    query_seq, key_seq, value_seq, attention_seq = (
        lax.all_gather(query_lin_delta, "ctx", axis=0, tiled=True),
        lax.all_gather(key_lin_delta, "ctx", axis=0, tiled=True),
        lax.all_gather(value_lin_delta, "ctx", axis=0, tiled=True),
        lax.all_gather(attention_low, "ctx", axis=0, tiled=True),
    )
    query_width = query_seq.shape[1] // ctx_count
    kv_width = key_seq.shape[1] // ctx_count
    query_bias_part = jnp.sum(
        lax.dynamic_slice_in_dim(query_seq, ctx_here * query_width, query_width, 1).astype(
            jnp.float32
        ),
        axis=0,
    )
    key_bias_part = jnp.sum(
        lax.dynamic_slice_in_dim(key_seq, ctx_here * kv_width, kv_width, 1).astype(jnp.float32),
        axis=0,
    )
    value_bias_part = jnp.sum(
        lax.dynamic_slice_in_dim(value_seq, ctx_here * kv_width, kv_width, 1).astype(jnp.float32),
        axis=0,
    )
    attn_parts = (
        lax.psum_scatter(
            inner(normed_cols, query_seq).astype(jnp.bfloat16),
            "fsdp",
            scatter_dimension=0,
            tiled=True,
        ).astype(jnp.float32),
        lax.psum_scatter(
            inner(normed_cols, key_seq).astype(jnp.bfloat16),
            "fsdp",
            scatter_dimension=0,
            tiled=True,
        ).astype(jnp.float32),
        lax.psum_scatter(
            inner(normed_cols, value_seq).astype(jnp.bfloat16),
            "fsdp",
            scatter_dimension=0,
            tiled=True,
        ).astype(jnp.float32),
        lax.psum_scatter(
            query_bias_part.astype(jnp.bfloat16), "fsdp", scatter_dimension=0, tiled=True
        ).astype(jnp.float32),
        lax.psum_scatter(
            key_bias_part.astype(jnp.bfloat16), "fsdp", scatter_dimension=0, tiled=True
        ).astype(jnp.float32),
        lax.psum_scatter(
            value_bias_part.astype(jnp.bfloat16), "fsdp", scatter_dimension=0, tiled=True
        ).astype(jnp.float32),
        lax.psum_scatter(
            inner(mixed_cols, attention_seq).astype(jnp.bfloat16),
            "fsdp",
            scatter_dimension=0,
            tiled=True,
        ).astype(jnp.float32),
    )
    gain_parts = (
        lax.psum_scatter(first_gain_delta, ("ctx", "fsdp"), scatter_dimension=0, tiled=True),
        lax.psum_scatter(second_gain_delta, ("ctx", "fsdp"), scatter_dimension=0, tiled=True),
    )
    return (
        layer_out,
        input_delta,
        gain_parts[0],
        attn_parts[0],
        attn_parts[1],
        attn_parts[2],
        attn_parts[3],
        attn_parts[4],
        attn_parts[5],
        attn_parts[6],
        gain_parts[1],
        gate_weight_delta,
        up_weight_delta,
        down_weight_delta,
    )


def solution(mesh):
    in_specs = (
        P(("fsdp", "ctx"), None),
        P("fsdp"),
        P(("ctx", "fsdp")),
        P(("ctx", "fsdp"), None),
        P(("ctx", "fsdp"), None),
        P(("ctx", "fsdp"), None),
        P(("ctx", "fsdp")),
        P(("ctx", "fsdp")),
        P(("ctx", "fsdp")),
        P(("ctx", "fsdp"), None),
        P(("ctx", "fsdp")),
        P(None, ("ctx", "fsdp")),
        P(None, ("ctx", "fsdp")),
        P(("ctx", "fsdp"), None),
        P(("fsdp", "ctx"), None),
    )
    out_specs = (
        P(("fsdp", "ctx"), None),
        P(("fsdp", "ctx"), None),
        P(("ctx", "fsdp")),
        P(("ctx", "fsdp"), None),
        P(("ctx", "fsdp"), None),
        P(("ctx", "fsdp"), None),
        P(("ctx", "fsdp")),
        P(("ctx", "fsdp")),
        P(("ctx", "fsdp")),
        P(("ctx", "fsdp"), None),
        P(("ctx", "fsdp")),
        P(None, ("ctx", "fsdp")),
        P(None, ("ctx", "fsdp")),
        P(("ctx", "fsdp"), None),
    )
    return jax.shard_map(local, mesh=mesh, in_specs=in_specs, out_specs=out_specs, check_vma=False)
```

profile of v0, /device:TPU:0, one launch (start us, length us, event | category | flops | bytes accessed | tf_op | source)
XLA Modules:
  0.0 1264.5 jit_solution(2949140065587778333)
XLA Ops:
  15.0 42.5 %all-reduce.15 = (bf16[1536]{0:T(1024)(128)(2,1)S(1)}, bf16[256]{0:T(256)(128)(2,1)S(1)}, bf16[256]{0:T(256)(128)(2,1)S(1)}, bf16[1536]{0:T(1024)(128)(2,1)S(1)}, bf16[1536]{0:T(1024)(128)(2,1)S(1)}) all-reduce(bf16[1536]{0:T(1024)(128)(2,1)S(1)} %dynamic-update-slice, ...), channel_id=1, replica_groups=mesh['ctx'=8,'fsdp'=4] {'ctx','fsdp'}, use_global_device_ids=true, to_apply=%add.4 | all-reduce | flops 5120 | bytes 20480
  58.2 77.9 %all_gather.61 = bf16[1536,256]{1,0:T(8,128)(2,1)S(1)} all-gather(bf16[48,256]{1,0:T(8,128)(2,1)S(1)} %copy-done.47), channel_id=1, replica_groups=mesh['ctx'=8,'fsdp'=4] {'ctx','fsdp'}, dimensions={0}, use_global_device_ids=true | all-gather | bytes 811008 | tf_op jit(solution)/shard_map/all_gather | solution.py:88
  137.3 10.1 all_gather.63
  149.0 80.3 %all_gather.64 = bf16[1536,256]{1,0:T(8,128)(2,1)S(1)} all-gather(bf16[48,256]{1,0:T(8,128)(2,1)S(1)} %copy-done.48), channel_id=1, replica_groups=mesh['ctx'=8,'fsdp'=4] {'ctx','fsdp'}, dimensions={0}, use_global_device_ids=true | all-gather | bytes 811008 | tf_op jit(solution)/shard_map/all_gather | solution.py:87
  232.1 8.5 all_gather.66
  242.2 4.5 convolution_add_fusion.3
  247.9 12.4 while.39
  260.9 11.5 while.40
  263.8 2.8 fusion.153
  269.4 3.1 fusion.153
  274.4 3.4 multiply_reduce_fusion.3
  277.9 45.9 %all-gather.14.cloned.1.call-done = bf16[1536,8960]{0,1:T(8,128)(2,1)} async-done(((bf16[1536,280]{0,1:T(8,128)(2,1)}), bf16[1536,8960]{0,1:T(8,128)(2,1)}) %all-gather.14.cloned.1.call-update) | async-done | bytes 27525136 | tf_op jit(solution)/shard_map/all_gather | solution.py:163
  323.8 16.4 %fusion.73 = f32[128,8960]{1,0:T(8,128)} fusion(bf16[128,1536]{1,0:T(8,128)(2,1)S(1)} %multiply_convert_fusion.3, bf16[1536,8960]{0,1:T(8,128)(2,1)} %all-gather.14.cloned.1.call-done), kind=kOutput, calls=%fused_computation.147 | convolution fusion | flops 3523215360 | bytes 32505856 | tf_op jit(solution)/shard_map/dot_general | solution.py:37
  340.2 150.4 %all-gather.16.cloned.1.call-done = bf16[1536,8960]{0,1:T(8,128)(2,1)} async-done(((bf16[1536,280]{0,1:T(8,128)(2,1)}), bf16[1536,8960]{0,1:T(8,128)(2,1)}) %all-gather.16.cloned.1.call-update) | async-done | bytes 27525136 | tf_op jit(solution)/shard_map/all_gather | solution.py:164
  490.6 16.2 %fusion.74 = f32[128,8960]{1,0:T(8,128)} fusion(bf16[128,1536]{1,0:T(8,128)(2,1)S(1)} %multiply_convert_fusion.3, bf16[1536,8960]{0,1:T(8,128)(2,1)} %all-gather.16.cloned.1.call-done), kind=kOutput, calls=%fused_computation.148 | convolution fusion | flops 3523215360 | bytes 32505856 | tf_op jit(solution)/shard_map/dot_general | solution.py:37
  506.8 150.6 %all-gather.18.cloned.1.call-done = bf16[8960,1536]{1,0:T(8,128)(2,1)} async-done(((bf16[280,1536]{1,0:T(8,128)(2,1)}), bf16[8960,1536]{1,0:T(8,128)(2,1)}) %all-gather.18.cloned.1.call-update) | async-done | bytes 27525136 | tf_op jit(solution)/shard_map/all_gather | solution.py:165
  657.4 17.9 %multiply_convert_fusion = (bf16[128,8960]{1,0:T(8,128)(2,1)S(1)}, bf16[128,8960]{1,0:T(8,128)(2,1)}, bf16[128,8960]{1,0:T(8,128)(2,1)}) fusion(f32[128,8960]{1,0:T(8,128)} %fusion.73, f32[128,8960]{1,0:T(8,128)} %fusion.74, bf16[128,1536]{1,0:T(8,128)(2,1)} %param.35, bf16[8960,1536]{1,0:T(8,128)(2,1)} %all-gather.18.cloned.1.call-done), kind=kOutput, calls=%fused_computation.65 | convolution fusion | flops 3543859200 | bytes 43974656 | tf_op jit(solution)/shard_map/dot_general | solution.py:37
  675.3 12.3 fusion.75
  687.6 11.6 multiply_reduce_fusion
  700.4 4.1 convolution_convert_fusion.6
  707.0 16.1 %while.41 = (s32[]{:T(128)}, f32[128,2,6,128]{0,3,2,1:T(8,128)S(1)}, f32[2,512,2,128]{3,1,2,0:T(8,128)}, bf16[2,512,2,128]{3,1,2,0:T(8,128)(2,1)}, bf16[2,512,2,...) while((s32[]{:T(128)}, ...), condition=%wide.region_11.12_spmd.clone, body=%wide.region_10.11_spmd.clone.sunk | while | flops 1014956032 | bytes 52390740 | solution.py:235
  732.6 3.5 all-to-all-start
  738.6 19.7 %reduce-scatter.10.cloned.1.call-done = bf16[128,256]{1,0:T(8,128)(2,1)} async-done(((bf16[1024,256]{1,0:T(8,128)(2,1)}), bf16[128,256]{1,0:T(8,128)(2,1)}) %reduce-scatter.10.cloned.1.call-update) | async-done | bytes 65552 | tf_op jit(solution)/shard_map/reduce_scatter | solution.py:241
  759.8 10.0 all_gather.75
  769.8 3.5 all-to-all-start.1
  774.3 22.2 %reduce-scatter.12.cloned.1.call-done = bf16[128,256]{1,0:T(8,128)(2,1)} async-done(((bf16[1024,256]{1,0:T(8,128)(2,1)}), bf16[128,256]{1,0:T(8,128)(2,1)}) %reduce-scatter.12.cloned.1.call-update) | async-done | bytes 65552 | tf_op jit(solution)/shard_map/reduce_scatter | solution.py:244
  796.5 10.8 all_gather.76
  807.3 3.6 all-to-all-start.2
  813.0 30.2 %all-gather.20.cloned.1.call-done = bf16[1024,1536]{0,1:T(8,128)(2,1)} async-done(((bf16[128,1536]{0,1:T(8,128)(2,1)}), bf16[1024,1536]{0,1:T(8,128)(2,1)}) %all-gather.20.cloned.1.call-update) | async-done | bytes 3145744 | tf_op jit(solution)/shard_map/all_gather | solution.py:278
  843.2 3.9 convolution_convert_fusion.5
  847.1 33.0 %all-gather.22.cloned.1.call-done = bf16[1024,1536]{1,0:T(8,128)(2,1)} async-done(((bf16[128,1536]{1,0:T(8,128)(2,1)}), bf16[1024,1536]{1,0:T(8,128)(2,1)}) %all-gather.22.cloned.1.call-update) | async-done | bytes 3145744 | tf_op jit(solution)/shard_map/all_gather | solution.py:281
  880.1 3.5 convolution_convert_fusion.4
  883.7 2.8 copy.87
  886.5 27.7 %all-gather.24.cloned.1.call-done = bf16[1024,1536]{1,0:T(8,128)(2,1)} async-done(((bf16[128,1536]{1,0:T(8,128)(2,1)}), bf16[1024,1536]{1,0:T(8,128)(2,1)}) %all-gather.24.cloned.1.call-update) | async-done | bytes 3145744 | tf_op jit(solution)/shard_map/all_gather | solution.py:183
  914.2 8.2 convolution_convert_fusion.3
  926.6 40.9 %all_to_all.92 = bf16[128,8,1120]{0,2,1:T(8,128)(2,1)S(1)} all-to-all(bf16[128,8,1120]{0,2,1:T(8,128)(2,1)} %bitcast.274), channel_id=1, replica_groups=mesh['ctx'=8,'fsdp'=4] {'ctx'}, dimensions={1} | all-to-all | bytes 4587520 | tf_op jit(solution)/shard_map/all_to_all | solution.py:179
  967.6 2.9 copy.89
  970.4 8.1 convolution_convert_fusion.2
  982.7 33.1 %all_to_all.93 = bf16[128,8,1120]{0,2,1:T(8,128)(2,1)} all-to-all(bf16[128,8,1120]{0,2,1:T(8,128)(2,1)} %bitcast.277), channel_id=1, replica_groups=mesh['ctx'=8,'fsdp'=4] {'ctx'}, dimensions={1} | all-to-all | bytes 4587520 | tf_op jit(solution)/shard_map/all_to_all | solution.py:180
  1015.7 4.4 copy.91
  1020.1 8.2 convolution_convert_fusion.1
  1030.9 4.0 fusion.76
  1034.9 12.0 fusion.51
  1048.0 42.3 %all-reduce.14 = (f32[1536]{0:T(1024)S(1)}, f32[1536]{0:T(1024)S(1)}) all-reduce(f32[1536]{0:T(1024)S(1)} %get-tuple-element.330, f32[1536]{0:T(1024)S(1)} %copy-done.46), channel_id=4, replica_groups=mesh['ctx'=8,'fsdp'=4] {'ctx','fsdp'}, use_global_device_ids=true, to_apply=%region_16.17.clone | all-reduce | flops 3072 | bytes 24576
  1099.1 11.6 all-reduce.16
  1115.1 5.0 reduce-scatter.22.cloned.1.call-done
  1122.6 64.7 %reduce-scatter.24.cloned.1.call-done = bf16[1536,280]{0,1:T(8,128)(2,1)} async-done(((bf16[1536,1120]{0,1:T(8,128)(2,1)}), bf16[1536,280]{0,1:T(8,128)(2,1)}) %reduce-scatter.24.cloned.1.call-update) | async-done | bytes 860176 | tf_op jit(solution)/shard_map/reduce_scatter | solution.py:193
  1189.9 64.7 %reduce-scatter.26.cloned.1.call-done = bf16[280,1536]{1,0:T(8,128)(2,1)} async-done(((bf16[1120,1536]{1,0:T(8,128)(2,1)}), bf16[280,1536]{1,0:T(8,128)(2,1)}) %reduce-scatter.26.cloned.1.call-update) | async-done | bytes 860176 | tf_op jit(solution)/shard_map/reduce_scatter | solution.py:196
  (312 shorter events, 103.8 us)
Async XLA Ops:
  7.2 50.3 %copy-start.11 = (bf16[128,1536]{1,0:T(8,128)(2,1)S(1)}, bf16[128,1536]{1,0:T(8,128)(2,1)}, u32[]{:S(2)}) copy-start(bf16[128,1536]{1,0:T(8,128)(2,1)} %param.21) | copy-start | bytes 1179652
  7.2 51.0 %copy-start.47 = (bf16[48,256]{1,0:T(8,128)(2,1)S(1)}, bf16[48,256]{1,0:T(8,128)(2,1)}, u32[]{:S(2)}) copy-start(bf16[48,256]{1,0:T(8,128)(2,1)} %param.26) | copy-start | bytes 73732
  7.2 235.0 %all-gather.10.cloned.1.call-start = ((), (), s32[]{:S(2)}) async-start(), calls=%async_computation.14 | async-start | bytes 4866048 | tf_op jit(solution)/shard_map/all_gather | solution.py:86
  7.9 266.4 %all-gather.12.cloned.1.call-start = ((), (), s32[]{:S(2)}) async-start(), calls=%async_computation.15 | async-start | bytes 4866048 | tf_op jit(solution)/shard_map/all_gather | solution.py:92
  8.7 315.1 %all-gather.14.cloned.1.call-start = ((), (), s32[]{:S(2)}) async-start(), calls=%async_computation.16 | async-start | bytes 28385280 | tf_op jit(solution)/shard_map/all_gather | solution.py:163
  9.4 139.0 %copy-start.51 = (s32[1024]{0:T(1024)S(1)}, s32[1024]{0:T(1024)}, u32[]{:S(2)}) copy-start(s32[1024]{0:T(1024)} %param.22) | copy-start | bytes 12292
  9.4 139.5 %copy-start.48 = (bf16[48,256]{1,0:T(8,128)(2,1)S(1)}, bf16[48,256]{1,0:T(8,128)(2,1)}, u32[]{:S(2)}) copy-start(bf16[48,256]{1,0:T(8,128)(2,1)} %param.25) | copy-start | bytes 73732
  9.4 481.2 %all-gather.16.cloned.1.call-start = ((), (), s32[]{:S(2)}) async-start(), calls=%async_computation.17 | async-start | bytes 28385280 | tf_op jit(solution)/shard_map/all_gather | solution.py:164
  10.0 647.4 %all-gather.18.cloned.1.call-start = ((), (), s32[]{:S(2)}) async-start(), calls=%async_computation.18 | async-start | bytes 28385280 | tf_op jit(solution)/shard_map/all_gather | solution.py:165
  10.6 747.8 %reduce-scatter.10.cloned.1.call-start = ((), (), s32[]{:S(2)}) async-start(), calls=%async_computation.19 | async-start | bytes 589824 | tf_op jit(solution)/shard_map/reduce_scatter | solution.py:241
  57.5 78.8 %copy-start.44 = (f32[1536]{0:T(1024)}, f32[1536]{0:T(1024)S(1)}, u32[]{:S(2)}) copy-start(f32[1536]{0:T(1024)S(1)} %convert_element_type.176) | copy-start | bytes 18436
  58.2 78.1 %copy-start.52 = (f32[128]{0:T(128)}, f32[128]{0:T(128)S(1)}, u32[]{:S(2)}) copy-start(f32[128]{0:T(128)S(1)} %fusion.69) | copy-start | bytes 1540
  137.0 105.2 %copy-start.14 = (bf16[128,1536]{1,0:T(8,128)(2,1)}, bf16[128,1536]{1,0:T(8,128)(2,1)S(1)}, u32[]{:S(2)}) copy-start(bf16[128,1536]{1,0:T(8,128)(2,1)S(1)} %fusion.55) | copy-start | bytes 1179652
  231.4 15.7 %copy-start.31 = (f32[128,64]{0,1:T(8,128)}, f32[128,64]{0,1:T(8,128)S(1)}, u32[]{:S(2)}) copy-start(f32[128,64]{0,1:T(8,128)S(1)} %get-tuple-element.411) | copy-start | bytes 98308
  231.4 15.7 %copy-start.33 = (f32[128,64]{0,1:T(8,128)}, f32[128,64]{0,1:T(8,128)S(1)}, u32[]{:S(2)}) copy-start(f32[128,64]{0,1:T(8,128)S(1)} %get-tuple-element.412) | copy-start | bytes 98308
  260.9 13.4 %copy-start.12 = (bf16[128,1536]{1,0:T(8,128)(2,1)S(1)}, bf16[128,1536]{1,0:T(8,128)(2,1)}, u32[]{:S(2)}) copy-start(bf16[128,1536]{1,0:T(8,128)(2,1)} %param.21) | copy-start | bytes 1179652
  277.7 421.5 %copy-start.4 = (f32[128,1536]{1,0:T(8,128)}, f32[128,1536]{1,0:T(8,128)S(1)}, u32[]{:S(2)}) copy-start(f32[128,1536]{1,0:T(8,128)S(1)} %get-tuple-element.414) | copy-start | bytes 2359300
  277.8 421.5 %copy-start.49 = (f32[128]{0:T(128)}, f32[128]{0:T(128)S(1)}, u32[]{:S(2)}) copy-start(f32[128]{0:T(128)S(1)} %fusion.70) | copy-start | bytes 1540
  277.9 212.7 %copy-start.15 = (bf16[128,1536]{1,0:T(8,128)(2,1)}, bf16[128,1536]{1,0:T(8,128)(2,1)S(1)}, u32[]{:S(2)}) copy-start(bf16[128,1536]{1,0:T(8,128)(2,1)S(1)} %multiply_convert_fusion.3) | copy-start | bytes 1179652
  687.6 12.5 copy-start.23
  725.9 70.6 %reduce-scatter.12.cloned.1.call-start = ((), (), s32[]{:S(2)}) async-start(), calls=%async_computation.20 | async-start | bytes 589824 | tf_op jit(solution)/shard_map/reduce_scatter | solution.py:244
  727.4 115.7 %all-gather.20.cloned.1.call-start = ((), (), s32[]{:S(2)}) async-start(), calls=%async_computation.21 | async-start | bytes 3538944 | tf_op jit(solution)/shard_map/all_gather | solution.py:278
  728.6 151.5 %all-gather.22.cloned.1.call-start = ((), (), s32[]{:S(2)}) async-start(), calls=%async_computation.25 | async-start | bytes 3538944 | tf_op jit(solution)/shard_map/all_gather | solution.py:281
  729.3 184.9 %all-gather.24.cloned.1.call-start = ((), (), s32[]{:S(2)}) async-start(), calls=%async_computation.27 | async-start | bytes 3538944 | tf_op jit(solution)/shard_map/all_gather | solution.py:183
  729.9 290.2 %all-gather.26.cloned.1.call-start = ((), (), s32[]{:S(2)}) async-start(), calls=%async_computation.30 | async-start | bytes 3538944 | tf_op jit(solution)/shard_map/all_gather | solution.py:184
  730.7 28.6 %copy-start.28 = (f32[128,64]{1,0:T(8,128)S(1)}, f32[128,64]{1,0:T(8,128)}, u32[]{:S(2)}) copy-start(f32[128,64]{1,0:T(8,128)} %copy-done.27) | copy-start | bytes 98308
  730.7 28.6 %copy-start.30 = (f32[128,64]{1,0:T(8,128)S(1)}, f32[128,64]{1,0:T(8,128)}, u32[]{:S(2)}) copy-start(f32[128,64]{1,0:T(8,128)} %copy-done.29) | copy-start | bytes 98308
  732.6 37.2 %all-to-all-start = ((bf16[128,8,192]{0,2,1:T(8,128)(2,1)}), bf16[128,8,192]{0,2,1:T(8,128)(2,1)S(1)}, u32[]{:S(2)}, u32[]{:S(2)}) async-start(bf16[128,8,192]{0,2,1:T(8,128)(2,1)} %bitcast.8), calls=%async_computation.2 | async-start | bytes 786432 | tf_op jit(solution)/shard_map/all_to_all | solution.py:274
  769.8 37.4 %copy-start.26 = (bf16[1024,256]{1,0:T(8,128)(2,1)}, bf16[1024,256]{1,0:T(8,128)(2,1)S(1)}, u32[]{:S(2)}) copy-start(bf16[1024,256]{1,0:T(8,128)(2,1)S(1)} %all_gather.75) | copy-start | bytes 1572868
  769.8 37.4 %all-to-all-start.1 = ((bf16[128,8,192]{0,2,1:T(8,128)(2,1)}), bf16[128,8,192]{0,2,1:T(8,128)(2,1)S(1)}, u32[]{:S(2)}, u32[]{:S(2)}) async-start(bf16[128,8,192]{0,2,1:T(8,128)(2,1)} %bitcast.10), calls=%async_computation.6 | async-start | bytes 786432 | tf_op jit(solution)/shard_map/all_to_all | solution.py:275
  773.3 321.9 %reduce-scatter.16.cloned.1.call-start = ((), (), s32[]{:S(2)}) async-start(), calls=%async_computation.23 | async-start | bytes 122880 | tf_op jit(solution)/shard_map/reduce_scatter | solution.py:306
  807.3 76.4 %all-to-all-start.2 = ((bf16[128,8,1120]{0,2,1:T(8,128)(2,1)}), bf16[128,8,1120]{0,2,1:T(8,128)(2,1)S(1)}, u32[]{:S(2)}, u32[]{:S(2)}) async-start(bf16[128,8,1120]{0,2,1:T(8,128)(2,1)} %bitcast.12), calls=%async_computation.8 | async-start | bytes 4587520 | tf_op jit(solution)/shard_map/all_to_all | solution.py:178
  810.9 285.7 %reduce-scatter.18.cloned.1.call-start = ((), (), s32[]{:S(2)}) async-start(), calls=%async_computation.24 | async-start | bytes 122880 | tf_op jit(solution)/shard_map/reduce_scatter | solution.py:312
  812.9 298.9 %reduce-scatter.14.cloned.1.call-start = ((), (), s32[]{:S(2)}) async-start(), calls=%async_computation.22 | async-start | bytes 737280 | tf_op jit(solution)/shard_map/reduce_scatter | solution.py:300
  847.1 266.4 %reduce-scatter.20.cloned.1.call-start = ((), (), s32[]{:S(2)}) async-start(), calls=%async_computation.26 | async-start | bytes 737280 | tf_op jit(solution)/shard_map/reduce_scatter | solution.py:327
  883.6 236.5 %reduce-scatter.22.cloned.1.call-start = ((), (), s32[]{:S(2)}) async-start(), calls=%async_computation.28 | async-start | bytes 4300800 | tf_op jit(solution)/shard_map/reduce_scatter | solution.py:187
  922.4 265.0 %reduce-scatter.24.cloned.1.call-start = ((), (), s32[]{:S(2)}) async-start(), calls=%async_computation.29 | async-start | bytes 4300800 | tf_op jit(solution)/shard_map/reduce_scatter | solution.py:193
  978.6 276.1 %reduce-scatter.26.cloned.1.call-start = ((), (), s32[]{:S(2)}) async-start(), calls=%async_computation.31 | async-start | bytes 4300800 | tf_op jit(solution)/shard_map/reduce_scatter | solution.py:196
  1034.9 12.5 copy-start.13
  1034.9 12.5 copy-start.19
  1034.9 12.5 copy-start.42
  1034.9 12.5 copy-start.45
  1046.9 46.9 %copy-start.58 = (f32[128]{0:T(128)S(1)}, f32[128]{0:T(128)}, u32[]{:S(2)}) copy-start(f32[128]{0:T(128)} %copy-done.57) | copy-start | bytes 1540
  1046.9 46.9 %copy-start.21 = (f32[128,1536]{1,0:T(8,128)S(1)}, f32[128,1536]{1,0:T(8,128)}, u32[]{:S(2)}) copy-start(f32[128,1536]{1,0:T(8,128)} %copy-done.20) | copy-start | bytes 2359300
  1046.9 46.9 %copy-start.24 = (bf16[128,1536]{1,0:T(8,128)(2,1)S(1)}, bf16[128,1536]{1,0:T(8,128)(2,1)}, u32[]{:S(2)}) copy-start(bf16[128,1536]{1,0:T(8,128)(2,1)} %param.35) | copy-start | bytes 1179652
  1047.0 46.9 %copy-start.50 = (f32[128]{0:T(128)S(1)}, f32[128]{0:T(128)}, u32[]{:S(2)}) copy-start(f32[128]{0:T(128)} %copy-done.49) | copy-start | bytes 1540
  1047.0 46.9 %copy-start.54 = (f32[128]{0:T(128)S(1)}, f32[128]{0:T(128)}, u32[]{:S(2)}) copy-start(f32[128]{0:T(128)} %copy-done.52) | copy-start | bytes 1540
  1047.0 46.9 %copy-start.56 = (f32[128]{0:T(128)S(1)}, f32[128]{0:T(128)}, u32[]{:S(2)}) copy-start(f32[128]{0:T(128)} %copy-done.55) | copy-start | bytes 1540
  (42 other events, 152.1 us)
Sparse Core Ops, SparseCore 0:
  10.8 69.2 all-gather.9
  82.9 63.1 all-gather.11
  148.9 174.8 all-gather.13
  326.5 164.0 all-gather.15
  493.3 164.0 all-gather.17
  726.1 32.2 reduce-scatter.9
  762.3 34.1 reduce-scatter.11
  798.4 44.7 all-gather.19
  845.0 35.0 all-gather.21
  881.8 32.3 all-gather.23
  916.1 49.2 all-gather.25
  968.1 19.1 reduce-scatter.15
  990.2 17.2 reduce-scatter.17
  1010.2 20.1 reduce-scatter.13
  1033.1 20.3 reduce-scatter.19
  1055.6 64.4 reduce-scatter.21
  1122.2 65.0 reduce-scatter.23
  1189.5 65.0 reduce-scatter.25
where the time goes:
time: 1270 us; the launch traced here: 1260 us
  waiting for transfers between devices  619 us (49%)
  blocking collectives  368 us (29%)
  matrix products  156 us (12%)
  local copies, waits for them, and re-layouts  54.6 us (4%)
  other arithmetic  37.4 us (3%)
  between operations  17 us (1%)
    all_gather x1, waiting for transfers between devices, local(): lax.all_gather(down_weight, ('ctx', 'fsdp'), axis=0, tiled=True)  151 us
    all_gather x1, waiting for transfers between devices, local(): lax.all_gather(up_weight, ('ctx', 'fsdp'), axis=1, tiled=True)  150 us
    dot_general x14, matrix products, matmul(): return jnp.dot(left, right, preferred_element_type=jnp.float32)  104 us
    unnamed x3, blocking collectives  96.4 us
    all_gather x1, blocking collectives, local(): lax.all_gather(key_weight, ('ctx', 'fsdp'), axis=0, tiled=True)  80.3 us
    all_gather x1, blocking collectives, local(): lax.all_gather(value_weight, ('ctx', 'fsdp'), axis=0, tiled=True)  77.9 us
    reduce_scatter x1, waiting for transfers between devices, local(): lax.psum_scatter(inner(normed_seq, up_cols).astype(jnp.bfloat16), 'fsdp',...  64.7 us
    reduce_scatter x1, waiting for transfers between devices, local(): lax.psum_scatter(inner(active_cols, cotangent_seq).astype(jnp.bfloat16),...  64.7 us
  transfers between devices with their start and end apart: 21, of which 11 were waited for; matrix products, arithmetic and copies ran while one was open for 13% of the time, Pallas kernels for 0%

commit v1 on v0

v1 whole, which is shorter than its diff:
```python
import jax
import jax.numpy as jnp
from jax import lax
from jax.sharding import Mesh
from jax.sharding import PartitionSpec as P

H = 12
KV = 2
HD = 128

epsilon = 1e-06
rope_base = 1000000.0
neg_large = -1e30

EVERY = ("grp", "core", "fsdp")
SEQ_AXES = ("grp", "core")
TP_AXES = ("fsdp", "core")


def rms_scale(values):
    return lax.rsqrt(jnp.mean(values * values, axis=-1, keepdims=True) + epsilon)


def rope_tables(places):
    half_width = HD // 2
    frequency = rope_base ** (-2.0 * jnp.arange(half_width, dtype=jnp.float32) / HD)
    angles = places.astype(jnp.float32)[:, None] * frequency[None, :]
    return jnp.cos(angles)[:, None, :], jnp.sin(angles)[:, None, :]


def rotate(values, cosine, sine):
    half_width = values.shape[-1] // 2
    leading = values[..., :half_width]
    trailing = values[..., half_width:]
    return jnp.concatenate(
        [leading * cosine - trailing * sine, trailing * cosine + leading * sine], axis=-1
    )


def matmul(left, right):
    return jnp.dot(left, right, preferred_element_type=jnp.float32)


def matmul_nt(left, right):
    return lax.dot_general(
        left, right, (((1,), (1,)), ((), ())), preferred_element_type=jnp.float32
    )


def inner(left, right):
    return lax.dot_general(
        left, right, (((0,), (0,)), ((), ())), preferred_element_type=jnp.float32
    )


def low(values):
    return values.astype(jnp.bfloat16)


def exchange(values, bit):
    count = lax.axis_size("grp")
    return lax.ppermute(values, "grp", [(i, i ^ bit) for i in range(count)])


def gather_group(block):
    count = lax.axis_size("grp")
    if count != 4:
        return lax.all_gather(block, "grp", axis=0, tiled=True)
    half = block.shape[1] // 2
    from_x = exchange(block, 1)
    from_y = exchange(block, 2)
    left = exchange(from_x[:, :half], 2)
    right = exchange(from_y[:, half:], 1)
    corner = jnp.concatenate([left, right], axis=1)
    return jnp.concatenate([block, from_x, from_y, corner], axis=0)


def scatter_group(parts):
    count = lax.axis_size("grp")
    if count != 4:
        return lax.psum_scatter(low(parts), "grp", scatter_dimension=0, tiled=True).astype(
            jnp.float32
        )
    rows = parts.shape[0] // 4
    half = parts.shape[1] // 2
    own, for_x, for_y, corner = (parts[i * rows : (i + 1) * rows] for i in range(4))
    corner = low(corner)
    from_x = exchange(corner[:, :half], 1).astype(jnp.float32)
    from_y = exchange(corner[:, half:], 2).astype(jnp.float32)
    for_y = jnp.concatenate([for_y[:, :half] + from_x, for_y[:, half:]], axis=1)
    for_x = jnp.concatenate([for_x[:, :half], for_x[:, half:] + from_y], axis=1)
    return (
        own
        + exchange(low(for_x), 1).astype(jnp.float32)
        + exchange(low(for_y), 2).astype(jnp.float32)
    )


def local(
    hidden,
    positions,
    first_gain,
    query_weight,
    key_weight,
    value_weight,
    query_bias,
    key_bias,
    value_bias,
    output_weight,
    second_gain,
    gate_weight,
    up_weight,
    down_weight,
    cotangent,
):
    rows = hidden.shape[0]
    width = hidden.shape[1]
    group_size = H // KV
    score_scale = HD ** (-0.5)
    ctx_here = lax.axis_index("grp") * lax.axis_size("core") + lax.axis_index("core")
    own_places = lax.dynamic_slice_in_dim(positions, ctx_here * rows, rows)
    q_width, k_width = H * HD, KV * HD

    projections = jnp.concatenate([query_weight, key_weight, value_weight], axis=1)
    weight_qkv = lax.all_gather(projections, EVERY, axis=0, tiled=True)
    small = jnp.concatenate([first_gain, second_gain, query_bias, key_bias, value_bias])
    small_all = lax.all_gather(small, EVERY, axis=0, tiled=False).astype(jnp.float32)
    own = width // small_all.shape[0]
    kv_own = k_width // small_all.shape[0]
    gain_one = small_all[:, :own].reshape(width)
    gain_two = small_all[:, own : 2 * own].reshape(width)
    bias_qkv = jnp.concatenate(
        [
            small_all[:, 2 * own : 3 * own].reshape(q_width),
            small_all[:, 3 * own : 3 * own + kv_own].reshape(k_width),
            small_all[:, 3 * own + kv_own :].reshape(k_width),
        ]
    )
    weight_output = lax.all_gather(output_weight, EVERY, axis=0, tiled=True)
    gate_rows = gather_group(gate_weight.T)
    up_rows = gather_group(up_weight.T)
    down_rows = gather_group(down_weight)
    cotangent_all = lax.all_gather(cotangent, TP_AXES, axis=0, tiled=True)

    inputs = hidden.astype(jnp.float32)
    unit_one = inputs * rms_scale(inputs)
    normed = low(unit_one * gain_one)
    lin = matmul(normed, weight_qkv) + bias_qkv
    cosine, sine = rope_tables(own_places)
    queries = low(rotate(lin[:, :q_width].reshape(rows, H, HD), cosine, sine)).reshape(
        rows, KV, group_size, HD
    )
    keys_local = low(
        rotate(lin[:, q_width : q_width + k_width].reshape(rows, KV, HD), cosine, sine)
    ).reshape(rows, k_width)
    values_local = low(lin[:, q_width + k_width :])
    kv_all = lax.all_gather(
        jnp.concatenate([keys_local, values_local], axis=1), SEQ_AXES, axis=0, tiled=True
    )
    length = kv_all.shape[0]
    keys = kv_all[:, :k_width].reshape(length, KV, HD)
    values = kv_all[:, k_width:].reshape(length, KV, HD)
    allowed = (positions[None, :] <= own_places[:, None])[None, None]

    scores = jnp.einsum("tgjd,sgd->gjts", queries, keys, preferred_element_type=jnp.float32)
    scores = jnp.where(allowed, scores * score_scale, neg_large)
    top = jnp.max(scores, axis=-1, keepdims=True)
    log_sum = top + jnp.log(jnp.sum(jnp.exp(scores - top), axis=-1, keepdims=True))
    probs = jnp.where(allowed, jnp.exp(scores - log_sum), 0.0)
    probs_low = low(probs)
    mixture = jnp.einsum("gjts,sgd->tgjd", probs_low, values, preferred_element_type=jnp.float32)
    mixed_low = low(mixture.reshape(rows, q_width))
    middle = inputs + matmul(mixed_low, weight_output)
    scale_two = rms_scale(middle)
    unit_two = middle * scale_two
    normed_two = low(unit_two * gain_two)

    normed_all = lax.all_gather(normed_two, TP_AXES, axis=0, tiled=True)
    gate = matmul_nt(normed_all, gate_rows)
    upward = matmul_nt(normed_all, up_rows)
    active_delta = low(matmul_nt(cotangent_all, down_rows)).astype(jnp.float32)
    sigmoid = 1.0 / (1.0 + jnp.exp(-gate))
    silu = gate * sigmoid
    active = low(silu * upward)
    gate_delta = low(active_delta * upward * (sigmoid * (1.0 + gate * (1.0 - sigmoid))))
    up_delta = low(active_delta * silu)
    normed_two_part = matmul(gate_delta, gate_rows) + matmul(up_delta, up_rows)
    normed_two_delta = lax.psum_scatter(
        low(normed_two_part), TP_AXES, scatter_dimension=0, tiled=True
    ).astype(jnp.float32)
    out_part = matmul(active, down_rows)
    out_sum = lax.psum_scatter(low(out_part), TP_AXES, scatter_dimension=0, tiled=True)
    layer_out = low(middle + out_sum.astype(jnp.float32))
    gate_grad = scatter_group(inner(gate_delta, normed_all)).T
    up_grad = scatter_group(inner(up_delta, normed_all)).T
    down_grad = scatter_group(inner(active, cotangent_all))

    second_gain_part = jnp.sum(normed_two_delta * unit_two, axis=0)
    scaled = normed_two_delta * gain_two
    middle_delta = cotangent.astype(jnp.float32) + scale_two * (
        scaled - unit_two * jnp.mean(scaled * unit_two, axis=-1, keepdims=True)
    )

    attention_low = low(middle_delta)
    output_grad = lax.psum_scatter(
        low(inner(mixed_low, attention_low)), EVERY, scatter_dimension=0, tiled=True
    ).astype(jnp.float32)
    mixed_delta = low(matmul_nt(attention_low, weight_output)).reshape(rows, KV, group_size, HD)
    row_dots = jnp.transpose(jnp.sum(mixed_delta.astype(jnp.float32) * mixture, axis=-1), (1, 2, 0))
    value_part = jnp.einsum(
        "gjts,tgjd->sgd", probs_low, mixed_delta, preferred_element_type=jnp.float32
    )
    prob_delta = jnp.einsum(
        "tgjd,sgd->gjts", mixed_delta, values, preferred_element_type=jnp.float32
    )
    score_delta = low(probs * (prob_delta - row_dots[..., None]))
    query_rot_delta = (
        jnp.einsum("gjts,sgd->tgjd", score_delta, keys, preferred_element_type=jnp.float32)
        * score_scale
    )
    key_part = (
        jnp.einsum("gjts,tgjd->sgd", score_delta, queries, preferred_element_type=jnp.float32)
        * score_scale
    )
    kv_part = jnp.concatenate(
        [key_part.reshape(length, k_width), value_part.reshape(length, k_width)], axis=1
    )
    kv_delta = lax.psum_scatter(low(kv_part), SEQ_AXES, scatter_dimension=0, tiled=True)
    key_lin_delta = low(
        rotate(
            kv_delta[:, :k_width].astype(jnp.float32).reshape(rows, KV, HD), cosine, -sine
        ).reshape(rows, k_width)
    )
    query_lin_delta = low(
        rotate(query_rot_delta.reshape(rows, H, HD), cosine, -sine).reshape(rows, q_width)
    )
    lin_delta = jnp.concatenate([query_lin_delta, key_lin_delta, kv_delta[:, k_width:]], axis=1)
    qkv_grad = lax.psum_scatter(
        low(inner(normed, lin_delta)), EVERY, scatter_dimension=0, tiled=True
    ).astype(jnp.float32)
    normed_delta = matmul_nt(lin_delta, weight_qkv)
    scale_one = rms_scale(inputs)
    first_gain_part = jnp.sum(normed_delta * unit_one, axis=0)
    scaled_one = normed_delta * gain_one
    input_delta = middle_delta + scale_one * (
        scaled_one - unit_one * jnp.mean(scaled_one * unit_one, axis=-1, keepdims=True)
    )

    bias_part = jnp.sum(lin_delta.astype(jnp.float32), axis=0)
    devices = small_all.shape[0]
    small_part = jnp.concatenate(
        [
            first_gain_part.reshape(devices, own),
            second_gain_part.reshape(devices, own),
            bias_part[:q_width].reshape(devices, own),
            bias_part[q_width : q_width + k_width].reshape(devices, kv_own),
            bias_part[q_width + k_width :].reshape(devices, kv_own),
        ],
        axis=1,
    )
    small_grad = lax.psum_scatter(small_part.reshape(-1), EVERY, scatter_dimension=0, tiled=True)
    return (
        layer_out,
        input_delta,
        small_grad[:own],
        qkv_grad[:, :q_width],
        qkv_grad[:, q_width : q_width + k_width],
        qkv_grad[:, q_width + k_width :],
        small_grad[2 * own : 3 * own],
        small_grad[3 * own : 3 * own + kv_own],
        small_grad[3 * own + kv_own :],
        output_grad,
        small_grad[own : 2 * own],
        gate_grad,
        up_grad,
        down_grad,
    )


def solution(mesh):
    cores = 2
    ctx, fsdp = mesh.shape["ctx"], mesh.shape["fsdp"]
    split = Mesh(mesh.devices.reshape(ctx // cores, cores, fsdp), EVERY)
    tokens = P(("fsdp", "grp", "core"), None)
    in_specs = (
        tokens,
        P("fsdp"),
        P(EVERY),
        P(EVERY, None),
        P(EVERY, None),
        P(EVERY, None),
        P(EVERY),
        P(EVERY),
        P(EVERY),
        P(EVERY, None),
        P(EVERY),
        P(None, EVERY),
        P(None, EVERY),
        P(EVERY, None),
        tokens,
    )
    out_specs = (
        tokens,
        tokens,
        P(EVERY),
        P(EVERY, None),
        P(EVERY, None),
        P(EVERY, None),
        P(EVERY),
        P(EVERY),
        P(EVERY),
        P(EVERY, None),
        P(EVERY),
        P(None, EVERY),
        P(None, EVERY),
        P(EVERY, None),
    )
    return jax.shard_map(local, mesh=split, in_specs=in_specs, out_specs=out_specs, check_vma=False)
```

time: 1270 us -> 697 us (0.55)
  blocking collectives: 368 us -> 82.1 us
  waiting for transfers between devices: 619 us -> 413 us
  matrix products: 156 us -> 105 us
  local copies, waits for them, and re-layouts: 54.6 us -> 24 us
  starting transfers between devices: 11.2 us -> 27 us
  other arithmetic: 37.4 us -> 21.9 us
    all_gather x9 -> x5, waiting for transfers between devices: 438 us -> 103 us  [the longest x1 57.8 us: local(): weight_output = lax.all_gather(output_weight, EVERY, axis=0, tiled=True)]
    all_gather x6 -> x0, blocking collectives: 198 us -> none  [the longest x1 80.3 us: local(): lax.all_gather(key_weight, ('ctx', 'fsdp'), axis=0, tiled=True)]
    ppermute x0 -> x24, waiting for transfers between devices: none -> 126 us  [exchange(): return lax.ppermute(values, 'grp', [(i, i ^ bit) for i in range(count)])]
    dot_general x14 -> x5, matrix products: 104 us -> 29.2 us  [matmul(): return jnp.dot(left, right, preferred_element_type=jnp.float32)]
    all_to_all x2 -> x0, blocking collectives: 74 us -> none  [the longest x1 40.9 us: local(): lax.all_to_all(up_low, 'ctx', split_axis=1, concat_axis=0, tiled=True)]
    dot_general x14 -> x11, matrix products: 17.4 us -> 48.2 us  [the longest x5 35.4 us: matmul_nt(): lax.dot_general(left, right, (((1,), (1,)), ((), ())), preferred_element_...]
    ppermute x0 -> x24, starting transfers between devices: none -> 26 us  [exchange(): return lax.ppermute(values, 'grp', [(i, i ^ bit) for i in range(count)])]
    convert_element_type x22 -> x3, other arithmetic: 21 us -> 3.3 us  [the longest x1 1.65 us: local(): output_grad = lax.psum_scatter(low(inner(mixed_low, attention_low)), EVER...]
  transfers between devices with their start and end apart: 21 -> 34, of which waited for: 11 -> 19; matrix products, arithmetic and copies ran while one was open for 13% -> 14% of each run, Pallas kernels for 0% -> 0%
where the time goes in v1:
time: 697 us; the launch traced here: 688 us
  waiting for transfers between devices  413 us (59%)
  matrix products  105 us (15%)
  blocking collectives  82.1 us (12%)
  starting transfers between devices  27 us (4%)
  local copies, waits for them, and re-layouts  24 us (3%)
  other arithmetic  21.9 us (3%)
  between operations  15.6 us (2%)
    ppermute x24, waiting for transfers between devices, exchange(): return lax.ppermute(values, 'grp', [(i, i ^ bit) for i in range(count)])  126 us
    reduce_scatter x1, waiting for transfers between devices, local(): lax.psum_scatter(low(inner(normed, lin_delta)), EVERY, scatter_dimension=...  91.5 us
    unnamed x2, blocking collectives  82.1 us
    all_gather x1, waiting for transfers between devices, local(): weight_output = lax.all_gather(output_weight, EVERY, axis=0, tiled=True)  57.8 us
    reduce_scatter x1, waiting for transfers between devices, local(): lax.psum_scatter(low(out_part), TP_AXES, scatter_dimension=0, tiled=True)  39.8 us
    dot_general x5, matrix products, matmul_nt(): lax.dot_general(left, right, (((1,), (1,)), ((), ())), preferred_element_...  35.4 us
    reduce_scatter x1, waiting for transfers between devices, local(): lax.psum_scatter(low(normed_two_part), TP_AXES, scatter_dimension=0, tile...  30.9 us
    dot_general x5, matrix products, matmul(): return jnp.dot(left, right, preferred_element_type=jnp.float32)  29.2 us
  transfers between devices with their start and end apart: 34, of which 19 were waited for; matrix products, arithmetic and copies ran while one was open for 14% of the time, Pallas kernels for 0%

profile of v1, /device:TPU:0, one launch (start us, length us, event | category | flops | bytes accessed | tf_op | source)
XLA Modules:
  0.0 688.5 jit_solution(7491264079416934719)
XLA Ops:
  7.2 1.6 pad_maximum_fusion.10
  8.9 3.4 concatenate.85
  12.6 42.5 %all-reduce = bf16[5120]{0:T(1024)(128)(2,1)S(1)} all-reduce(bf16[5120]{0:T(1024)(128)(2,1)S(1)} %dynamic-update-slice), channel_id=2, replica_groups=mesh['grp'=4,'core'=2,'fsdp'=4] {'grp','core','fsdp'}, use_global_device_ids=true, to_apply=%add | all-reduce | flops 5120 | bytes 20480
  58.1 26.0 %all-gather.7.cloned.1.call-done = bf16[1536,2048]{1,0:T(8,128)(2,1)} async-done(((bf16[48,2048]{1,0:T(8,128)(2,1)}), bf16[1536,2048]{1,0:T(8,128)(2,1)}) %all-gather.7.cloned.1.call-update) | async-done | bytes 6291472 | tf_op jit(solution)/shard_map/all_gather | solution.py:125
  84.1 4.0 convolution_add_fusion.1
  92.0 19.5 %all-gather.9.cloned.1.call-done = bf16[1024,512]{1,0:T(8,128)(2,1)} async-done(((bf16[128,512]{1,0:T(8,128)(2,1)}), bf16[1024,512]{1,0:T(8,128)(2,1)}) %all-gather.9.cloned.1.call-update) | async-done | bytes 1048592 | tf_op jit(solution)/shard_map/all_gather | solution.py:157
  117.6 2.5 fusion.68
  120.1 57.8 %all-gather.11.cloned.1.call-done = bf16[1536,1536]{1,0:T(8,128)(2,1)} async-done(((bf16[48,1536]{1,0:T(8,128)(2,1)}), bf16[1536,1536]{1,0:T(8,128)(2,1)}) %all-gather.11.cloned.1.call-update) | async-done | bytes 4718608 | tf_op jit(solution)/shard_map/all_gather | solution.py:139
  177.9 3.2 multiply_reduce_fusion.1
  182.3 1.5 collective-permute-start.8
  187.9 16.6 %collective-permute-done.8 = bf16[280,1536]{1,0:T(8,128)(2,1)S(1)} collective-permute-done((bf16[280,1536]{1,0:T(8,128)(2,1)}, bf16[280,1536]{1,0:T(8,128)(2,1)S(1)}, u32[]{:S(2)}, u32[]{:S(2)}) %collective-permute-start.8) | collective-permute-done | bytes 860192 | tf_op jit(solution)/shard_map/ppermute | solution.py:62
  207.0 17.5 %collective-permute-done.1 = bf16[280,1536]{1,0:T(8,128)(2,1)S(1)} collective-permute-done((bf16[280,1536]{1,0:T(8,128)(2,1)}, bf16[280,1536]{1,0:T(8,128)(2,1)S(1)}, u32[]{:S(2)}, u32[]{:S(2)}) %collective-permute-start.1) | collective-permute-done | bytes 860192 | tf_op jit(solution)/shard_map/ppermute | solution.py:62
  225.1 1.5 collective-permute-start.3
  227.4 15.5 %collective-permute-done.5 = bf16[280,1536]{1,0:T(8,128)(2,1)S(1)} collective-permute-done((bf16[280,1536]{1,0:T(8,128)(2,1)}, bf16[280,1536]{1,0:T(8,128)(2,1)S(1)}, u32[]{:S(2)}, u32[]{:S(2)}) %collective-permute-start.5) | collective-permute-done | bytes 860192 | tf_op jit(solution)/shard_map/ppermute | solution.py:62
  246.6 5.5 collective-permute-done.10
  252.9 8.2 %convolution_convert_fusion.2 = bf16[1120,1024]{1,0:T(8,128)(2,1)} fusion(bf16[1024,1536]{1,0:T(8,128)(2,1)} %all-gather.15.cloned.1.call-done, bf16[280,768]{1,0:T(8,128)(2,1)} %collective-permute-done.11, bf16[280,768]{1,0:T(8,128)(2,1)} %copy-done.41, bf16[280,1536]{1,0:T(8,128)(2,1)} %copy-done.19, bf16[280,1536]{1,0:T(8,128)(2,1)} %copy-done.17, ...), kind=kOutput, calls=%fused_computation.19 | convolution fusion | flops 3541565440 | bytes 8880128 | tf_op jit(solution)/shard_map/dot_general | solution.py:45
  261.5 7.9 %fusion.52 = f32[1024,1120]{0,1:T(8,128)S(1)} fusion(bf16[1024,1536]{1,0:T(8,128)(2,1)} %all-gather.13.cloned.1.call-done, bf16[280,768]{1,0:T(8,128)(2,1)} %collective-permute-done.3, bf16[280,768]{1,0:T(8,128)(2,1)} %collective-permute-done.2, bf16[280,1536]{1,0:T(8,128)(2,1)S(1)} %copy-done.22, bf16[280,1536]{1,0:T(8,128)(2,1)} %copy-done.24, ...), kind=kOutput, calls=%fused_computation.125 | convolution fusion | flops 3540418560 | bytes 11173888 | tf_op jit(solution)/shard_map/dot_general | solution.py:45
  269.7 9.3 %fusion.4 = (bf16[1024,1120]{0,1:T(8,128)(2,1)S(1)}, bf16[1024,1120]{0,1:T(8,128)(2,1)}, bf16[1024,1120]{0,1:T(8,128)(2,1)S(1)}) fusion(bf16[1120,1024]{1,0:T(8,128)(2,1)S(1)} %copy-done.45, f32[1024,1120]{0,1:T(8,128)S(1)} %fusion.52, bf16[1024,1536]{1,0:T(8,128)(2,1)S(1)} %copy-done.37, bf16[280,768]{1,0:T(8,128)(2,1)} %collective-permute-done.7, ...), kind=kOutput, calls=%fused_computation.13 | convolution fusion | flops 3558768640 | bytes 20348928 | tf_op jit(solution)/shard_map/dot_general | solution.py:45
  279.1 6.3 fusion.50
  285.4 7.6 %add_convert_fusion = bf16[1024,1536]{1,0:T(8,128)(2,1)} fusion(f32[1024,1536]{1,0:T(8,128)S(1)} %fusion.50, bf16[1024,1120]{0,1:T(8,128)(2,1)S(1)} %get-tuple-element.20, bf16[280,768]{1,0:T(8,128)(2,1)} %collective-permute-done.3, bf16[280,768]{1,0:T(8,128)(2,1)} %collective-permute-done.2, bf16[280,1536]{1,0:T(8,128)(2,1)S(1)} %copy-done.23, ...), kind=kOutput, calls=%fused_computation.6 | convolution fusion | flops 3543564288 | bytes 15171584 | tf_op jit(solution)/shard_map/dot_general | solution.py:41
  293.2 8.1 %convolution_convert_fusion.3 = bf16[1024,1536]{1,0:T(8,128)(2,1)} fusion(bf16[1024,1120]{0,1:T(8,128)(2,1)} %get-tuple-element.21, bf16[280,768]{1,0:T(8,128)(2,1)} %collective-permute-done.11, bf16[280,768]{1,0:T(8,128)(2,1)} %copy-done.41, bf16[280,1536]{1,0:T(8,128)(2,1)S(1)} %copy-done.20, bf16[280,1536]{1,0:T(8,128)(2,1)S(1)} %copy-done.18, ...), kind=kOutput, calls=%fused_computation.20 | convolution fusion | flops 3541991424 | bytes 8880128 | tf_op jit(solution)/shard_map/dot_general | solution.py:41
  301.5 30.9 %reduce-scatter.10.cloned.1.call-done = bf16[128,1536]{1,0:T(8,128)(2,1)} async-done(((bf16[1024,1536]{1,0:T(8,128)(2,1)}), bf16[128,1536]{1,0:T(8,128)(2,1)}) %reduce-scatter.10.cloned.1.call-update) | async-done | bytes 393232 | tf_op jit(solution)/shard_map/reduce_scatter | solution.py:188
  332.4 1.9 fusion.31
  334.3 39.8 %reduce-scatter.8.cloned.1.call-done = bf16[128,1536]{1,0:T(8,128)(2,1)} async-done(((bf16[1024,1536]{1,0:T(8,128)(2,1)}), bf16[128,1536]{1,0:T(8,128)(2,1)}) %reduce-scatter.8.cloned.1.call-update) | async-done | bytes 393232 | tf_op jit(solution)/shard_map/reduce_scatter | solution.py:192
  374.0 2.2 fusion.30
  376.2 4.9 convolution_convert_fusion.4
  381.1 1.9 copy.74
  383.0 4.7 fusion.15
  387.9 2.4 fusion.1
  390.3 1.6 copy-done.1
  394.6 3.6 convolution_convert_fusion.1
  398.6 9.3 %fusion.71 = (bf16[1120,1536]{1,0:T(8,128)(2,1)S(1)}, f32[1120,1536]{1,0:T(8,128)}) fusion(bf16[1024,1120]{0,1:T(8,128)(2,1)} %get-tuple-element.21, bf16[1024,1536]{1,0:T(8,128)(2,1)} %all-gather.15.cloned.1.call-done), kind=kOutput, calls=%fused_computation.142 | convolution fusion | flops 3524935680 | bytes 15761408 | tf_op jit(solution)/shard_map/dot_general | solution.py:51
  412.7 20.0 %reduce-scatter.16.cloned.1.call-done = bf16[128,512]{1,0:T(8,128)(2,1)} async-done(((bf16[1024,512]{1,0:T(8,128)(2,1)}), bf16[128,512]{1,0:T(8,128)(2,1)}) %reduce-scatter.16.cloned.1.call-update) | async-done | bytes 131088
  434.6 4.5 convolution_convert_fusion
  439.1 6.5 fusion.69
  447.8 3.7 fusion.70
  456.7 1.9 collective-permute-done.14
  461.0 6.8 collective-permute-done.18
  470.5 17.1 %collective-permute-done.23 = bf16[280,1536]{1,0:T(8,128)(2,1)S(1)} collective-permute-done((bf16[280,1536]{1,0:T(8,128)(2,1)S(1)}, bf16[280,1536]{1,0:T(8,128)(2,1)S(1)}, u32[]{:S(2)}, u32[]{:S(2)}) %collective-permute-start.23) | collective-permute-done | bytes 860192 | tf_op jit(solution)/shard_map/ppermute | solution.py:62
  489.8 24.8 %collective-permute-done.15 = bf16[280,1536]{1,0:T(8,128)(2,1)S(1)} collective-permute-done((bf16[280,1536]{1,0:T(8,128)(2,1)S(1)}, bf16[280,1536]{1,0:T(8,128)(2,1)S(1)}, u32[]{:S(2)}, u32[]{:S(2)}) %collective-permute-start.15) | collective-permute-done | bytes 860192 | tf_op jit(solution)/shard_map/ppermute | solution.py:62
  514.5 1.5 fusion.12
  516.0 19.5 %collective-permute-done.19 = bf16[280,1536]{1,0:T(8,128)(2,1)S(1)} collective-permute-done((bf16[280,1536]{1,0:T(8,128)(2,1)S(1)}, bf16[280,1536]{1,0:T(8,128)(2,1)S(1)}, u32[]{:S(2)}, u32[]{:S(2)}) %collective-permute-start.19) | collective-permute-done | bytes 860192 | tf_op jit(solution)/shard_map/ppermute | solution.py:62
  535.6 1.5 fusion.10
  537.1 5.1 fusion.37
  543.0 39.5 %all-reduce.1 = f32[5120]{0:T(1024)S(1)} all-reduce(f32[5120]{0:T(1024)S(1)} %reshape.265), channel_id=6, replica_groups=mesh['grp'=4,'core'=2,'fsdp'=4] {'grp','core','fsdp'}, use_global_device_ids=true, to_apply=%region_13.14.clone | all-reduce | flops 5120 | bytes 40960
  585.0 1.6 convert_element_type.182
  586.6 91.5 %reduce-scatter.12.cloned.1.call-done = bf16[48,2048]{1,0:T(8,128)(2,1)} async-done(((bf16[1536,2048]{1,0:T(8,128)(2,1)}), bf16[48,2048]{1,0:T(8,128)(2,1)}) %reduce-scatter.12.cloned.1.call-update) | async-done | bytes 196624 | tf_op jit(solution)/shard_map/reduce_scatter | solution.py:238
  679.5 1.6 slice.320
  (253 shorter events, 56.4 us)
Async XLA Ops:
  7.2 76.9 %all-gather.7.cloned.1.call-start = ((), (), s32[]{:S(2)}) async-start(), calls=%async_computation.5 | async-start | bytes 6488064 | tf_op jit(solution)/shard_map/all_gather | solution.py:125
  8.9 102.6 %all-gather.9.cloned.1.call-start = ((), (), s32[]{:S(2)}) async-start(), calls=%async_computation.6 | async-start | bytes 1179648 | tf_op jit(solution)/shard_map/all_gather | solution.py:157
  58.1 30.0 %copy-start.33 = (f32[128]{0:T(128)}, f32[128]{0:T(128)S(1)}, u32[]{:S(2)}) copy-start(f32[128]{0:T(128)S(1)} %add_rsqrt_fusion.1) | copy-start | bytes 1540
  58.1 32.7 %copy-start.35 = (s32[1024]{0:T(1024)S(1)}, s32[1024]{0:T(1024)}, u32[]{:S(2)}) copy-start(s32[1024]{0:T(1024)} %param.16) | copy-start | bytes 12292
  89.4 88.5 %all-gather.11.cloned.1.call-start = ((), (), s32[]{:S(2)}) async-start(), calls=%async_computation.7 | async-start | bytes 4866048 | tf_op jit(solution)/shard_map/all_gather | solution.py:139
  90.1 162.8 %all-gather.15.cloned.1.call-start = ((), (), s32[]{:S(2)}) async-start(), calls=%async_computation.10 | async-start | bytes 3538944 | tf_op jit(solution)/shard_map/all_gather | solution.py:143
  90.7 170.8 %all-gather.13.cloned.1.call-start = ((), (), s32[]{:S(2)}) async-start(), calls=%async_computation.8 | async-start | bytes 3538944 | tf_op jit(solution)/shard_map/all_gather | solution.py:178
  91.7 23.2 %copy-start.6 = (bf16[128,12,64]{2,0,1:T(8,128)(2,1)}, bf16[128,12,64]{2,0,1:T(8,128)(2,1)S(1)}, u32[]{:S(2)}) copy-start(bf16[128,12,64]{2,0,1:T(8,128)(2,1)S(1)} %copy.69) | copy-start | bytes 589828
  92.0 23.0 %copy-start.8 = (bf16[128,12,64]{2,0,1:T(8,128)(2,1)}, bf16[128,12,64]{2,0,1:T(8,128)(2,1)S(1)}, u32[]{:S(2)}) copy-start(bf16[128,12,64]{2,0,1:T(8,128)(2,1)S(1)} %copy.70) | copy-start | bytes 589828
  117.6 60.4 %copy-start.3 = (bf16[128,1536]{1,0:T(8,128)(2,1)S(1)}, bf16[128,1536]{1,0:T(8,128)(2,1)}, u32[]{:S(2)}) copy-start(bf16[128,1536]{1,0:T(8,128)(2,1)} %param.15) | copy-start | bytes 1179652
  120.1 86.9 %copy-start.10 = (bf16[128,2,6,128]{0,3,2,1:T(8,128)(2,1)}, bf16[128,2,6,128]{0,3,2,1:T(8,128)(2,1)S(1)}, u32[]{:S(2)}) copy-start(bf16[128,2,6,128]{0,3,2,1:T(8,128)(2,1)S(1)} %get-tuple-element.76) | copy-start | bytes 1179652
  181.2 151.2 %copy-start.36 = (f32[128]{0:T(128)}, f32[128]{0:T(128)S(1)}, u32[]{:S(2)}) copy-start(f32[128]{0:T(128)S(1)} %add_rsqrt_fusion) | copy-start | bytes 1540
  182.1 150.3 %reduce-scatter.10.cloned.1.call-start = ((), (), s32[]{:S(2)}) async-start(), calls=%async_computation.11 | async-start | bytes 3538944 | tf_op jit(solution)/shard_map/reduce_scatter | solution.py:188
  182.3 22.2 %collective-permute-start.8 = (bf16[280,1536]{1,0:T(8,128)(2,1)}, bf16[280,1536]{1,0:T(8,128)(2,1)S(1)}, u32[]{:S(2)}, u32[]{:S(2)}) collective-permute-start(bf16[280,1536]{1,0:T(8,128)(2,1)} %param.28), channel_id=1, source_target_pairs={{0,8},{8,0},{16,24},{24,16},{1,9},{9,1},{17,25},{25,17},{2,10},{10... | collective-permute-start | bytes 2580488 | tf_op jit(solution)/shard_map/ppermute | solution.py:62
  183.8 22.2 %collective-permute-start.9 = (bf16[280,1536]{1,0:T(8,128)(2,1)}, bf16[280,1536]{1,0:T(8,128)(2,1)S(1)}, u32[]{:S(2)}, u32[]{:S(2)}) collective-permute-start(bf16[280,1536]{1,0:T(8,128)(2,1)} %param.28), channel_id=1, source_target_pairs={{0,16},{8,24},{16,0},{24,8},{1,17},{9,25},{17,1},{25,9},{2,18},{10... | collective-permute-start | bytes 2580488 | tf_op jit(solution)/shard_map/ppermute | solution.py:62
  184.4 40.0 %collective-permute-start.1 = (bf16[280,1536]{1,0:T(8,128)(2,1)}, bf16[280,1536]{1,0:T(8,128)(2,1)S(1)}, u32[]{:S(2)}, u32[]{:S(2)}) collective-permute-start(bf16[280,1536]{1,0:T(8,128)(2,1)} %bitcast.137), channel_id=1, source_target_pairs={{0,16},{8,24},{16,0},{24,8},{1,17},{9,25},{17,1},{25,9},{2,18},{10... | collective-permute-start | bytes 2580488 | tf_op jit(solution)/shard_map/ppermute | solution.py:62
  185.9 39.2 %collective-permute-start = (bf16[280,1536]{1,0:T(8,128)(2,1)}, bf16[280,1536]{1,0:T(8,128)(2,1)S(1)}, u32[]{:S(2)}, u32[]{:S(2)}) collective-permute-start(bf16[280,1536]{1,0:T(8,128)(2,1)} %bitcast.138), channel_id=1, source_target_pairs={{0,8},{8,0},{16,24},{24,16},{1,9},{9,1},{17,25},{25,17},{2,10},{10... | collective-permute-start | bytes 2580488 | tf_op jit(solution)/shard_map/ppermute | solution.py:62
  186.5 56.4 %collective-permute-start.5 = (bf16[280,1536]{1,0:T(8,128)(2,1)}, bf16[280,1536]{1,0:T(8,128)(2,1)S(1)}, u32[]{:S(2)}, u32[]{:S(2)}) collective-permute-start(bf16[280,1536]{1,0:T(8,128)(2,1)} %bitcast.133), channel_id=1, source_target_pairs={{0,16},{8,24},{16,0},{24,8},{1,17},{9,25},{17,1},{25,9},{2,18},{10... | collective-permute-start | bytes 2580488 | tf_op jit(solution)/shard_map/ppermute | solution.py:62
  204.6 39.8 %collective-permute-start.4 = (bf16[280,1536]{1,0:T(8,128)(2,1)}, bf16[280,1536]{1,0:T(8,128)(2,1)S(1)}, u32[]{:S(2)}, u32[]{:S(2)}) collective-permute-start(bf16[280,1536]{1,0:T(8,128)(2,1)} %bitcast.134), channel_id=1, source_target_pairs={{0,8},{8,0},{16,24},{24,16},{1,9},{9,1},{17,25},{25,17},{2,10},{10... | collective-permute-start | bytes 2580488 | tf_op jit(solution)/shard_map/ppermute | solution.py:62
  206.1 46.1 %copy-start.19 = (bf16[280,1536]{1,0:T(8,128)(2,1)}, bf16[280,1536]{1,0:T(8,128)(2,1)S(1)}, u32[]{:S(2)}) copy-start(bf16[280,1536]{1,0:T(8,128)(2,1)S(1)} %collective-permute-done.9) | copy-start | bytes 2580484
  206.1 46.1 %collective-permute-start.10 = (bf16[280,768]{1,0:T(8,128)(2,1)S(1)}, bf16[280,768]{1,0:T(8,128)(2,1)S(1)}, u32[]{:S(2)}, u32[]{:S(2)}) collective-permute-start(bf16[280,768]{1,0:T(8,128)(2,1)S(1)} %slice.309), channel_id=1, source_target_pairs={{0,16},{8,24},{16,0},{24,8},{1,17},{9,25},{17,1},{25,9},{2,18},{10... | collective-permute-start | bytes 1290248 | tf_op jit(solution)/shard_map/ppermute | solution.py:62
  224.5 28.3 %copy-start.21 = (bf16[280,1536]{1,0:T(8,128)(2,1)}, bf16[280,1536]{1,0:T(8,128)(2,1)S(1)}, u32[]{:S(2)}) copy-start(bf16[280,1536]{1,0:T(8,128)(2,1)S(1)} %collective-permute-done.1) | copy-start | bytes 2580484
  224.5 28.4 %collective-permute-start.11 = (bf16[280,768]{1,0:T(8,128)(2,1)S(1)}, bf16[280,768]{1,0:T(8,128)(2,1)}, u32[]{:S(2)}, u32[]{:S(2)}) collective-permute-start(bf16[280,768]{1,0:T(8,128)(2,1)S(1)} %slice.310), channel_id=1, source_target_pairs={{0,8},{8,0},{16,24},{24,16},{1,9},{9,1},{17,25},{25,17},{2,10},{10... | collective-permute-start | bytes 1290248 | tf_op jit(solution)/shard_map/ppermute | solution.py:62
  225.1 27.6 %copy-start.24 = (bf16[280,1536]{1,0:T(8,128)(2,1)}, bf16[280,1536]{1,0:T(8,128)(2,1)S(1)}, u32[]{:S(2)}) copy-start(bf16[280,1536]{1,0:T(8,128)(2,1)S(1)} %collective-permute-done) | copy-start | bytes 2580484
  225.1 36.0 %collective-permute-start.3 = (bf16[280,768]{1,0:T(8,128)(2,1)S(1)}, bf16[280,768]{1,0:T(8,128)(2,1)}, u32[]{:S(2)}, u32[]{:S(2)}) collective-permute-start(bf16[280,768]{1,0:T(8,128)(2,1)S(1)} %slice.306), channel_id=1, source_target_pairs={{0,8},{8,0},{16,24},{24,16},{1,9},{9,1},{17,25},{25,17},{2,10},{10... | collective-permute-start | bytes 1290248 | tf_op jit(solution)/shard_map/ppermute | solution.py:62
  242.9 18.5 %collective-permute-start.2 = (bf16[280,768]{1,0:T(8,128)(2,1)}, bf16[280,768]{1,0:T(8,128)(2,1)}, u32[]{:S(2)}, u32[]{:S(2)}) collective-permute-start(bf16[280,768]{1,0:T(8,128)(2,1)} %slice.305), channel_id=1, source_target_pairs={{0,16},{8,24},{16,0},{24,8},{1,17},{9,25},{17,1},{25,9},{2,18},{10... | collective-permute-start | bytes 1290248 | tf_op jit(solution)/shard_map/ppermute | solution.py:62
  244.3 25.1 %collective-permute-start.7 = (bf16[280,768]{1,0:T(8,128)(2,1)}, bf16[280,768]{1,0:T(8,128)(2,1)}, u32[]{:S(2)}, u32[]{:S(2)}) collective-permute-start(bf16[280,768]{1,0:T(8,128)(2,1)} %slice.308), channel_id=1, source_target_pairs={{0,8},{8,0},{16,24},{24,16},{1,9},{9,1},{17,25},{25,17},{2,10},{10... | collective-permute-start | bytes 1290248 | tf_op jit(solution)/shard_map/ppermute | solution.py:62
  252.1 17.6 %collective-permute-start.6 = (bf16[280,768]{1,0:T(8,128)(2,1)}, bf16[280,768]{1,0:T(8,128)(2,1)}, u32[]{:S(2)}, u32[]{:S(2)}) collective-permute-start(bf16[280,768]{1,0:T(8,128)(2,1)} %slice.307), channel_id=1, source_target_pairs={{0,16},{8,24},{16,0},{24,8},{1,17},{9,25},{17,1},{25,9},{2,18},{10... | collective-permute-start | bytes 1290248 | tf_op jit(solution)/shard_map/ppermute | solution.py:62
  293.0 81.0 %reduce-scatter.8.cloned.1.call-start = ((), (), s32[]{:S(2)}) async-start(), calls=%async_computation.9 | async-start | bytes 3538944 | tf_op jit(solution)/shard_map/reduce_scatter | solution.py:192
  301.4 72.6 %copy-start.13 = (bf16[128,1536]{1,0:T(8,128)(2,1)S(1)}, bf16[128,1536]{1,0:T(8,128)(2,1)}, u32[]{:S(2)}) copy-start(bf16[128,1536]{1,0:T(8,128)(2,1)} %param.29) | copy-start | bytes 1179652
  301.4 131.3 %reduce-scatter.16.cloned.1.call-start = ((), (), s32[]{:S(2)}) async-start(), calls=%async_computation.14 | async-start | bytes 1179648
  394.6 190.4 %reduce-scatter.14.cloned.1.call-start = ((), (), s32[]{:S(2)}) async-start(), calls=%async_computation.13 | async-start | bytes 4866048 | tf_op jit(solution)/shard_map/reduce_scatter | solution.py:205
  398.2 279.9 %reduce-scatter.12.cloned.1.call-start = ((), (), s32[]{:S(2)}) async-start(), calls=%async_computation.12 | async-start | bytes 6488064 | tf_op jit(solution)/shard_map/reduce_scatter | solution.py:238
  398.6 13.3 %copy-start.2 = (bf16[2,6,128,1024]{2,3,1,0:T(8,128)(2,1)S(1)}, bf16[2,6,128,1024]{2,3,1,0:T(8,128)(2,1)}, u32[]{:S(2)}) copy-start(bf16[2,6,128,1024]{2,3,1,0:T(8,128)(2,1)} %copy-done.1) | copy-start | bytes 9437188
  408.9 25.6 %copy-start.34 = (f32[128]{0:T(128)S(1)}, f32[128]{0:T(128)}, u32[]{:S(2)}) copy-start(f32[128]{0:T(128)} %copy-done.33) | copy-start | bytes 1540
  408.9 44.2 %collective-permute-start.22 = (bf16[280,768]{1,0:T(8,128)(2,1)}, bf16[280,768]{1,0:T(8,128)(2,1)}, u32[]{:S(2)}, u32[]{:S(2)}) collective-permute-start(bf16[280,768]{1,0:T(8,128)(2,1)} %get-tuple-element.31), channel_id=1, source_target_pairs={{0,8},{8,0},{16,24},{24,16},{1,9},{9,1},{17,25},{25,17},{2,10},{10... | collective-permute-start | bytes 1290248 | tf_op jit(solution)/shard_map/ppermute | solution.py:62
  410.4 43.3 %collective-permute-start.20 = (bf16[280,768]{1,0:T(8,128)(2,1)}, bf16[280,768]{1,0:T(8,128)(2,1)}, u32[]{:S(2)}, u32[]{:S(2)}) collective-permute-start(bf16[280,768]{1,0:T(8,128)(2,1)} %get-tuple-element.32), channel_id=1, source_target_pairs={{0,16},{8,24},{16,0},{24,8},{1,17},{9,25},{17,1},{25,9},{2,18},{10... | collective-permute-start | bytes 1290248 | tf_op jit(solution)/shard_map/ppermute | solution.py:62
  445.7 12.9 %collective-permute-start.14 = (bf16[280,768]{1,0:T(8,128)(2,1)S(1)}, bf16[280,768]{1,0:T(8,128)(2,1)S(1)}, u32[]{:S(2)}, u32[]{:S(2)}) collective-permute-start(bf16[280,768]{1,0:T(8,128)(2,1)S(1)} %get-tuple-element.39), channel_id=1, source_target_pairs={{0,8},{8,0},{16,24},{24,16},{1,9},{9,1},{17,25},{25,17},{2,10},{10... | collective-permute-start | bytes 1290248 | tf_op jit(solution)/shard_map/ppermute | solution.py:62
  447.2 12.8 %collective-permute-start.12 = (bf16[280,768]{1,0:T(8,128)(2,1)S(1)}, bf16[280,768]{1,0:T(8,128)(2,1)S(1)}, u32[]{:S(2)}, u32[]{:S(2)}) collective-permute-start(bf16[280,768]{1,0:T(8,128)(2,1)S(1)} %get-tuple-element.40), channel_id=1, source_target_pairs={{0,16},{8,24},{16,0},{24,8},{1,17},{9,25},{17,1},{25,9},{2,18},{10... | collective-permute-start | bytes 1290248 | tf_op jit(solution)/shard_map/ppermute | solution.py:62
  451.6 16.1 %collective-permute-start.18 = (bf16[280,768]{1,0:T(8,128)(2,1)S(1)}, bf16[280,768]{1,0:T(8,128)(2,1)S(1)}, u32[]{:S(2)}, u32[]{:S(2)}) collective-permute-start(bf16[280,768]{1,0:T(8,128)(2,1)S(1)} %get-tuple-element.35), channel_id=1, source_target_pairs={{0,8},{8,0},{16,24},{24,16},{1,9},{9,1},{17,25},{25,17},{2,10},{10... | collective-permute-start | bytes 1290248 | tf_op jit(solution)/shard_map/ppermute | solution.py:62
  453.1 16.3 %collective-permute-start.16 = (bf16[280,768]{1,0:T(8,128)(2,1)S(1)}, bf16[280,768]{1,0:T(8,128)(2,1)S(1)}, u32[]{:S(2)}, u32[]{:S(2)}) collective-permute-start(bf16[280,768]{1,0:T(8,128)(2,1)S(1)} %get-tuple-element.36), channel_id=1, source_target_pairs={{0,16},{8,24},{16,0},{24,8},{1,17},{9,25},{17,1},{25,9},{2,18},{10... | collective-permute-start | bytes 1290248 | tf_op jit(solution)/shard_map/ppermute | solution.py:62
  455.2 32.5 %collective-permute-start.23 = (bf16[280,1536]{1,0:T(8,128)(2,1)S(1)}, bf16[280,1536]{1,0:T(8,128)(2,1)S(1)}, u32[]{:S(2)}, u32[]{:S(2)}) collective-permute-start(bf16[280,1536]{1,0:T(8,128)(2,1)S(1)} %pad_maximum_fusion.6), channel_id=1, source_target_pairs={{0,16},{8,24},{16,0},{24,8},{1,17},{9,25},{17,1},{25,9},{2,18},{10... | collective-permute-start | bytes 2580488 | tf_op jit(solution)/shard_map/ppermute | solution.py:62
  458.6 29.7 %collective-permute-start.21 = (bf16[280,1536]{1,0:T(8,128)(2,1)S(1)}, bf16[280,1536]{1,0:T(8,128)(2,1)S(1)}, u32[]{:S(2)}, u32[]{:S(2)}) collective-permute-start(bf16[280,1536]{1,0:T(8,128)(2,1)S(1)} %pad_maximum_fusion.5), channel_id=1, source_target_pairs={{0,8},{8,0},{16,24},{24,16},{1,9},{9,1},{17,25},{25,17},{2,10},{10... | collective-permute-start | bytes 2580488 | tf_op jit(solution)/shard_map/ppermute | solution.py:62
  460.3 54.2 %collective-permute-start.15 = (bf16[280,1536]{1,0:T(8,128)(2,1)S(1)}, bf16[280,1536]{1,0:T(8,128)(2,1)S(1)}, u32[]{:S(2)}, u32[]{:S(2)}) collective-permute-start(bf16[280,1536]{1,0:T(8,128)(2,1)S(1)} %pad_maximum_fusion.2), channel_id=1, source_target_pairs={{0,16},{8,24},{16,0},{24,8},{1,17},{9,25},{17,1},{25,9},{2,18},{10... | collective-permute-start | bytes 2580488 | tf_op jit(solution)/shard_map/ppermute | solution.py:62
  467.8 46.8 %collective-permute-start.13 = (bf16[280,1536]{1,0:T(8,128)(2,1)S(1)}, bf16[280,1536]{1,0:T(8,128)(2,1)S(1)}, u32[]{:S(2)}, u32[]{:S(2)}) collective-permute-start(bf16[280,1536]{1,0:T(8,128)(2,1)S(1)} %pad_maximum_fusion.1), channel_id=1, source_target_pairs={{0,8},{8,0},{16,24},{24,16},{1,9},{9,1},{17,25},{25,17},{2,10},{10... | collective-permute-start | bytes 2580488 | tf_op jit(solution)/shard_map/ppermute | solution.py:62
  469.8 65.8 %collective-permute-start.19 = (bf16[280,1536]{1,0:T(8,128)(2,1)S(1)}, bf16[280,1536]{1,0:T(8,128)(2,1)S(1)}, u32[]{:S(2)}, u32[]{:S(2)}) collective-permute-start(bf16[280,1536]{1,0:T(8,128)(2,1)S(1)} %pad_maximum_fusion.4), channel_id=1, source_target_pairs={{0,16},{8,24},{16,0},{24,8},{1,17},{9,25},{17,1},{25,9},{2,18},{10... | collective-permute-start | bytes 2580488 | tf_op jit(solution)/shard_map/ppermute | solution.py:62
  487.7 47.9 %collective-permute-start.17 = (bf16[280,1536]{1,0:T(8,128)(2,1)S(1)}, bf16[280,1536]{1,0:T(8,128)(2,1)S(1)}, u32[]{:S(2)}, u32[]{:S(2)}) collective-permute-start(bf16[280,1536]{1,0:T(8,128)(2,1)S(1)} %pad_maximum_fusion.3), channel_id=1, source_target_pairs={{0,8},{8,0},{16,24},{24,16},{1,9},{9,1},{17,25},{25,17},{2,10},{10... | collective-permute-start | bytes 2580488 | tf_op jit(solution)/shard_map/ppermute | solution.py:62
  489.8 47.3 %copy-start.30 = (f32[1536]{0:T(1024)S(1)}, f32[1536]{0:T(1024)}, u32[]{:S(2)}) copy-start(f32[1536]{0:T(1024)} %get-tuple-element.14) | copy-start | bytes 18436
  (36 other events, 223.4 us)
Sparse Core Ops, SparseCore 0:
  11.5 72.5 all-gather.6
  89.5 21.9 all-gather.8
  114.3 63.5 all-gather.10
  179.4 37.0 all-gather.14
  218.6 37.1 all-gather.12
  293.1 39.1 reduce-scatter.9
  334.7 39.3 reduce-scatter.7
  394.7 37.9 reduce-scatter.15
  438.2 120.0 reduce-scatter.13
  564.7 113.4 reduce-scatter.11

commit v2 on v1

--- a/solution.py
+++ b/solution.py
@@ -57,15 +57,27 @@
     return values.astype(jnp.bfloat16)
 
 
+def after(values, *others):
+    return lax.optimization_barrier((values, others))[0]
+
+
 def exchange(values, bit):
     count = lax.axis_size("grp")
     return lax.ppermute(values, "grp", [(i, i ^ bit) for i in range(count)])
 
 
+def other_core(values):
+    return lax.ppermute(values, "core", [(0, 1), (1, 0)])
+
+
 def gather_group(block):
     count = lax.axis_size("grp")
     if count != 4:
-        return lax.all_gather(block, "grp", axis=0, tiled=True)
+        bit = 1
+        while bit < count:
+            block = jnp.concatenate([block, exchange(block, bit)], axis=0)
+            bit *= 2
+        return block
     half = block.shape[1] // 2
     from_x = exchange(block, 1)
     from_y = exchange(block, 2)
@@ -75,25 +87,90 @@
     return jnp.concatenate([block, from_x, from_y, corner], axis=0)
 
 
-def scatter_group(parts):
+def scatter_group(parts, *before):
     count = lax.axis_size("grp")
+    rows = parts.shape[0] // count
     if count != 4:
-        return lax.psum_scatter(low(parts), "grp", scatter_dimension=0, tiled=True).astype(
-            jnp.float32
-        )
-    rows = parts.shape[0] // 4
+        bit = count // 2
+        parts = parts.astype(jnp.float32)
+        while bit:
+            keep, give = parts[: bit * rows], parts[bit * rows :]
+            parts = keep + exchange(low(give), bit).astype(jnp.float32)
+            bit //= 2
+        return after(parts, *before)
     half = parts.shape[1] // 2
-    own, for_x, for_y, corner = (parts[i * rows : (i + 1) * rows] for i in range(4))
+    own, for_x, for_y, corner = (
+        parts[i * rows : (i + 1) * rows].astype(jnp.float32) for i in range(4)
+    )
     corner = low(corner)
     from_x = exchange(corner[:, :half], 1).astype(jnp.float32)
     from_y = exchange(corner[:, half:], 2).astype(jnp.float32)
     for_y = jnp.concatenate([for_y[:, :half] + from_x, for_y[:, half:]], axis=1)
     for_x = jnp.concatenate([for_x[:, :half], for_x[:, half:] + from_y], axis=1)
-    return (
-        own
-        + exchange(low(for_x), 1).astype(jnp.float32)
-        + exchange(low(for_y), 2).astype(jnp.float32)
-    )
+    from_x = after(exchange(low(for_x), 1), *before).astype(jnp.float32)
+    from_y = after(exchange(low(for_y), 2), *before).astype(jnp.float32)
+    return own + from_x + from_y
+
+
+def gather_sequence(block):
+    mine = gather_group(block)
+    return jnp.concatenate([mine, other_core(mine)], axis=0)
+
+
+def scatter_sequence(parts):
+    half = parts.shape[0] // 2
+    return scatter_group(
+        parts[:half].astype(jnp.float32) + other_core(low(parts[half:])).astype(jnp.float32)
+    )
+
+
+def sequence_order(values):
+    count = lax.axis_size("grp")
+    ctx = lax.axis_index("grp") * 2 + lax.axis_index("core")
+    rows = values.shape[0] // (2 * count)
+    return jnp.concatenate(
+        [
+            lax.dynamic_slice_in_dim(values, (ctx ^ (2 * i + j)) * rows, rows)
+            for j in range(2)
+            for i in range(count)
+        ]
+    )
+
+
+def swap_groups(values):
+    count = lax.axis_size("grp")
+    if count == 1:
+        return values
+    width = values.shape[1] // count
+    grp = lax.axis_index("grp")
+    return jnp.concatenate(
+        [lax.dynamic_slice_in_dim(values, (grp ^ i) * width, width, 1) for i in range(count)],
+        axis=1,
+    )
+
+
+def swap_halves(values):
+    half = values.shape[1] // 2
+    first = lax.axis_index("core") == 0
+    left, right = values[:, :half], values[:, half:]
+    return jnp.where(first, left, right), jnp.where(first, right, left)
+
+
+def gather_weight(block, *before):
+    rows = after(lax.all_gather(block, ("core", "fsdp"), axis=0, tiled=True), *before)
+    half = rows.shape[1] // 2
+    mine = gather_group(lax.dynamic_slice_in_dim(rows, lax.axis_index("core") * half, half, 1))
+    return mine, other_core(mine)
+
+
+def sum_everywhere(values):
+    for axis in ("core", "grp", "fsdp"):
+        count = lax.axis_size(axis)
+        bit = 1
+        while bit < count:
+            values = values + lax.ppermute(values, axis, [(i, i ^ bit) for i in range(count)])
+            bit *= 2
+    return values
 
 
 def local(
@@ -122,11 +199,21 @@
     q_width, k_width = H * HD, KV * HD
 
     projections = jnp.concatenate([query_weight, key_weight, value_weight], axis=1)
-    weight_qkv = lax.all_gather(projections, EVERY, axis=0, tiled=True)
     small = jnp.concatenate([first_gain, second_gain, query_bias, key_bias, value_bias])
-    small_all = lax.all_gather(small, EVERY, axis=0, tiled=False).astype(jnp.float32)
-    own = width // small_all.shape[0]
-    kv_own = k_width // small_all.shape[0]
+    devices = lax.axis_size(EVERY)
+    device_here = lax.axis_index(EVERY)
+    small_all = sum_everywhere(
+        lax.dynamic_update_slice_in_dim(
+            jnp.zeros((devices, small.shape[0]), jnp.float32),
+            small.astype(jnp.float32)[None],
+            device_here,
+            0,
+        )
+    )
+    down_rows = gather_group(down_weight)
+    qkv_mine, qkv_other = gather_weight(projections, small_all, down_rows)
+    own = width // devices
+    kv_own = k_width // devices
     gain_one = small_all[:, :own].reshape(width)
     gain_two = small_all[:, own : 2 * own].reshape(width)
     bias_qkv = jnp.concatenate(
@@ -136,16 +223,19 @@
             small_all[:, 3 * own + kv_own :].reshape(k_width),
         ]
     )
-    weight_output = lax.all_gather(output_weight, EVERY, axis=0, tiled=True)
+    output_mine, output_other = gather_weight(output_weight)
     gate_rows = gather_group(gate_weight.T)
     up_rows = gather_group(up_weight.T)
-    down_rows = gather_group(down_weight)
     cotangent_all = lax.all_gather(cotangent, TP_AXES, axis=0, tiled=True)
 
     inputs = hidden.astype(jnp.float32)
     unit_one = inputs * rms_scale(inputs)
     normed = low(unit_one * gain_one)
-    lin = matmul(normed, weight_qkv) + bias_qkv
+    normed_swapped = swap_groups(normed)
+    lin_halves = jnp.concatenate(
+        [matmul(normed_swapped, qkv_mine), matmul(normed_swapped, qkv_other)], axis=1
+    )
+    lin = jnp.concatenate(swap_halves(lin_halves), axis=1) + bias_qkv
     cosine, sine = rope_tables(own_places)
     queries = low(rotate(lin[:, :q_width].reshape(rows, H, HD), cosine, sine)).reshape(
         rows, KV, group_size, HD
@@ -154,13 +244,16 @@
         rotate(lin[:, q_width : q_width + k_width].reshape(rows, KV, HD), cosine, sine)
     ).reshape(rows, k_width)
     values_local = low(lin[:, q_width + k_width :])
-    kv_all = lax.all_gather(
-        jnp.concatenate([keys_local, values_local], axis=1), SEQ_AXES, axis=0, tiled=True
-    )
+    kv_all = gather_sequence(jnp.concatenate([keys_local, values_local], axis=1))
     length = kv_all.shape[0]
+    places = positions.reshape(-1, rows)
+    steps = jnp.arange(places.shape[0], dtype=jnp.int32)
+    from_ctx = ctx_here ^ jnp.concatenate([steps[0::2], steps[1::2]])
+    matches = from_ctx[:, None] == jnp.arange(places.shape[0], dtype=jnp.int32)[None, :]
+    key_places = jnp.sum(jnp.where(matches[:, :, None], places[None], 0), axis=1).reshape(length)
     keys = kv_all[:, :k_width].reshape(length, KV, HD)
     values = kv_all[:, k_width:].reshape(length, KV, HD)
-    allowed = (positions[None, :] <= own_places[:, None])[None, None]
+    allowed = (key_places[None, :] <= own_places[:, None])[None, None]
 
     scores = jnp.einsum("tgjd,sgd->gjts", queries, keys, preferred_element_type=jnp.float32)
     scores = jnp.where(allowed, scores * score_scale, neg_large)
@@ -170,7 +263,11 @@
     probs_low = low(probs)
     mixture = jnp.einsum("gjts,sgd->tgjd", probs_low, values, preferred_element_type=jnp.float32)
     mixed_low = low(mixture.reshape(rows, q_width))
-    middle = inputs + matmul(mixed_low, weight_output)
+    mixed_swapped = swap_groups(mixed_low)
+    attention_halves = jnp.concatenate(
+        [matmul(mixed_swapped, output_mine), matmul(mixed_swapped, output_other)], axis=1
+    )
+    middle = inputs + jnp.concatenate(swap_halves(attention_halves), axis=1)
     scale_two = rms_scale(middle)
     unit_two = middle * scale_two
     normed_two = low(unit_two * gain_two)
@@ -190,10 +287,9 @@
     ).astype(jnp.float32)
     out_part = matmul(active, down_rows)
     out_sum = lax.psum_scatter(low(out_part), TP_AXES, scatter_dimension=0, tiled=True)
-    layer_out = low(middle + out_sum.astype(jnp.float32))
-    gate_grad = scatter_group(inner(gate_delta, normed_all)).T
-    up_grad = scatter_group(inner(up_delta, normed_all)).T
-    down_grad = scatter_group(inner(active, cotangent_all))
+    gate_grad_sums = inner(gate_delta, normed_all)
+    up_grad_sums = inner(up_delta, normed_all)
+    down_grad_sums = inner(active, cotangent_all)
 
     second_gain_part = jnp.sum(normed_two_delta * unit_two, axis=0)
     scaled = normed_two_delta * gain_two
@@ -202,10 +298,10 @@
     )
 
     attention_low = low(middle_delta)
-    output_grad = lax.psum_scatter(
-        low(inner(mixed_low, attention_low)), EVERY, scatter_dimension=0, tiled=True
-    ).astype(jnp.float32)
-    mixed_delta = low(matmul_nt(attention_low, weight_output)).reshape(rows, KV, group_size, HD)
+    low_mine, low_other = swap_halves(attention_low)
+    mixed_delta = low(
+        swap_groups(matmul_nt(low_mine, output_mine) + matmul_nt(low_other, output_other))
+    ).reshape(rows, KV, group_size, HD)
     row_dots = jnp.transpose(jnp.sum(mixed_delta.astype(jnp.float32) * mixture, axis=-1), (1, 2, 0))
     value_part = jnp.einsum(
         "gjts,tgjd->sgd", probs_low, mixed_delta, preferred_element_type=jnp.float32
@@ -225,7 +321,7 @@
     kv_part = jnp.concatenate(
         [key_part.reshape(length, k_width), value_part.reshape(length, k_width)], axis=1
     )
-    kv_delta = lax.psum_scatter(low(kv_part), SEQ_AXES, scatter_dimension=0, tiled=True)
+    kv_delta = low(scatter_sequence(kv_part))
     key_lin_delta = low(
         rotate(
             kv_delta[:, :k_width].astype(jnp.float32).reshape(rows, KV, HD), cosine, -sine
@@ -235,22 +331,45 @@
         rotate(query_rot_delta.reshape(rows, H, HD), cosine, -sine).reshape(rows, q_width)
     )
     lin_delta = jnp.concatenate([query_lin_delta, key_lin_delta, kv_delta[:, k_width:]], axis=1)
-    qkv_grad = lax.psum_scatter(
-        low(inner(normed, lin_delta)), EVERY, scatter_dimension=0, tiled=True
-    ).astype(jnp.float32)
-    normed_delta = matmul_nt(lin_delta, weight_qkv)
+    delta_mine, delta_other = swap_halves(lin_delta)
+    normed_delta = swap_groups(
+        matmul_nt(delta_mine, qkv_mine) + matmul_nt(delta_other, qkv_other)
+    )
     scale_one = rms_scale(inputs)
-    first_gain_part = jnp.sum(normed_delta * unit_one, axis=0)
     scaled_one = normed_delta * gain_one
     input_delta = middle_delta + scale_one * (
         scaled_one - unit_one * jnp.mean(scaled_one * unit_one, axis=-1, keepdims=True)
     )
 
+    def columns(values):
+        return sequence_order(
+            lax.all_to_all(values, SEQ_AXES, split_axis=1, concat_axis=0, tiled=True)
+        )
+
+    output_grad = lax.psum_scatter(
+        low(inner(columns(mixed_low), gather_sequence(attention_low))),
+        "fsdp",
+        scatter_dimension=0,
+        tiled=True,
+    ).astype(jnp.float32)
+    qkv_grad = lax.psum_scatter(
+        low(inner(columns(normed), gather_sequence(lin_delta))),
+        "fsdp",
+        scatter_dimension=0,
+        tiled=True,
+    ).astype(jnp.float32)
+    first_gain_grad = jnp.sum(
+        qkv_grad * projections.astype(jnp.float32), axis=1
+    ) / first_gain.astype(jnp.float32)
+
+    gate_grad = scatter_group(gate_grad_sums, lin_delta).T
+    up_grad = scatter_group(up_grad_sums, lin_delta).T
+    down_grad = scatter_group(down_grad_sums, lin_delta)
+    layer_out = low(middle + after(out_sum, lin_delta).astype(jnp.float32))
+
     bias_part = jnp.sum(lin_delta.astype(jnp.float32), axis=0)
-    devices = small_all.shape[0]
     small_part = jnp.concatenate(
         [
-            first_gain_part.reshape(devices, own),
             second_gain_part.reshape(devices, own),
             bias_part[:q_width].reshape(devices, own),
             bias_part[q_width : q_width + k_width].reshape(devices, kv_own),
@@ -258,19 +377,19 @@
         ],
         axis=1,
     )
-    small_grad = lax.psum_scatter(small_part.reshape(-1), EVERY, scatter_dimension=0, tiled=True)
+    small_grad = lax.dynamic_slice_in_dim(sum_everywhere(small_part), device_here, 1, 0)[0]
     return (
         layer_out,
         input_delta,
-        small_grad[:own],
+        first_gain_grad,
         qkv_grad[:, :q_width],
         qkv_grad[:, q_width : q_width + k_width],
         qkv_grad[:, q_width + k_width :],
-        small_grad[2 * own : 3 * own],
-        small_grad[3 * own : 3 * own + kv_own],
-        small_grad[3 * own + kv_own :],
+        small_grad[own : 2 * own],
+        small_grad[2 * own : 2 * own + kv_own],
+        small_grad[2 * own + kv_own :],
         output_grad,
-        small_grad[own : 2 * own],
+        small_grad[:own],
         gate_grad,
         up_grad,
         down_grad,

time: 697 us -> 595 us (0.85)
  waiting for transfers between devices: 413 us -> 169 us
  local copies, waits for them, and re-layouts: 24 us -> 127 us
  blocking collectives: 82.1 us -> 0 us
  other arithmetic: 21.9 us -> 81.6 us
  starting transfers between devices: 27 us -> 76.1 us
  matrix products: 105 us -> 117 us
    all_gather x3 -> x2, waiting for transfers between devices: 103 us -> 5.4 us  [gather_weight(): lax.all_gather(block, ('core', 'fsdp'), axis=0, tiled=True)]
    unnamed x2 -> x0, blocking collectives: 82.1 us -> none
    reduce_scatter x2, waiting for transfers between devices: 91.5 us -> 16.1 us  [the longest x1 16.1 us: local(): lax.psum_scatter(low(inner(columns(normed), gather_sequence(lin_delta))),...]
    reduce_scatter x1, waiting for transfers between devices: 39.8 us -> 0.01 us  [local(): lax.psum_scatter(low(out_part), TP_AXES, scatter_dimension=0, tiled=True)]
    reduce_scatter x1, waiting for transfers between devices: 30.9 us -> 0.01 us  [local(): lax.psum_scatter(low(normed_two_part), TP_AXES, scatter_dimension=0, tile...]
    unnamed x109 -> x176, local copies, waits for them, and re-layouts: 5.34 us -> 35.7 us
    ppermute x24 -> x48, starting transfers between devices: 26 us -> 51.6 us  [exchange(): return lax.ppermute(values, 'grp', [(i, i ^ bit) for i in range(count)])]
    concatenate x2 -> x7, other arithmetic: 1.71 us -> 27 us  [the longest x5 26.1 us: gather_group(): return jnp.concatenate([block, from_x, from_y, corner], axis=0)]
  transfers between devices with their start and end apart: 34 -> 74, of which waited for: 19 -> 28; matrix products, arithmetic and copies ran while one was open for 14% -> 49% of each run, Pallas kernels for 0% -> 0%
where the time goes in v2:
time: 595 us; the launch traced here: 586 us
  waiting for transfers between devices  169 us (28%)
  local copies, waits for them, and re-layouts  127 us (21%)
  matrix products  117 us (20%)
  other arithmetic  81.6 us (14%)
  starting transfers between devices  76.1 us (13%)
  between operations  15.6 us (3%)
    ppermute x48, waiting for transfers between devices, exchange(): return lax.ppermute(values, 'grp', [(i, i ^ bit) for i in range(count)])  104 us
    ppermute x48, starting transfers between devices, exchange(): return lax.ppermute(values, 'grp', [(i, i ^ bit) for i in range(count)])  51.6 us
    dot_general x7, matrix products, matmul_nt(): lax.dot_general(left, right, (((1,), (1,)), ((), ())), preferred_element_...  37.5 us
    unnamed x176, local copies, waits for them, and re-layouts  35.7 us
    dot_general x7, matrix products, matmul(): return jnp.dot(left, right, preferred_element_type=jnp.float32)  30.9 us
    dot_general x5, matrix products, inner(): lax.dot_general(left, right, (((0,), (0,)), ((), ())), preferred_element_...  29 us
    concatenate x5, other arithmetic, gather_group(): return jnp.concatenate([block, from_x, from_y, corner], axis=0)  26.1 us
    all_to_all x2, waiting for transfers between devices, columns(): lax.all_to_all(values, SEQ_AXES, split_axis=1, concat_axis=0, tiled=True)  24.7 us
  transfers between devices with their start and end apart: 74, of which 28 were waited for; matrix products, arithmetic and copies ran while one was open for 49% of the time, Pallas kernels for 0%

profile of v2, /device:TPU:0, one launch (start us, length us, event | category | flops | bytes accessed | tf_op | source)
XLA Modules:
  0.0 585.7 jit_solution(5489083021202077657)
XLA Ops:
  12.7 2.9 collective-permute-start.1
  23.5 3.4 collective-permute-done.3
  29.1 4.7 collective-permute-done.4
  34.4 5.4 all-gather.5.cloned.1.call-done
  44.1 16.6 %collective-permute-done.10 = bf16[384,1024]{1,0:T(8,128)(2,1)S(1)} collective-permute-done((bf16[384,1024]{1,0:T(8,128)(2,1)S(1)}, bf16[384,1024]{1,0:T(8,128)(2,1)S(1)}, u32[]{:S(2)}, u32[]{:S(2)}) %collective-permute-start.10) | collective-permute-done | bytes 786464 | tf_op jit(solution)/shard_map/ppermute | solution.py:66
  64.0 7.4 %collective-permute-done.12 = bf16[384,512]{1,0:T(8,128)(2,1)S(1)} collective-permute-done((bf16[384,512]{1,0:T(8,128)(2,1)S(1)}, bf16[384,512]{1,0:T(8,128)(2,1)S(1)}, u32[]{:S(2)}, u32[]{:S(2)}) %collective-permute-start.12) | collective-permute-done | bytes 393248 | tf_op jit(solution)/shard_map/ppermute | solution.py:66
  72.7 9.2 %maximum_maximum_fusion.3 = bf16[1536,1024]{1,0:T(8,128)(2,1)S(1)} fusion(bf16[384,512]{1,0:T(8,128)(2,1)S(1)} %collective-permute-done.12, bf16[384,512]{1,0:T(8,128)(2,1)S(1)} %collective-permute-done.11, bf16[384,1024]{1,0:T(8,128)(2,1)} %copy-done.18, bf16[384,1024]{1,0:T(8,128)(2,1)} %copy-done.19, bf16[384,1024]{1,0:T(8,128)(2,1)} %copy-done.13), kind=kLoop, calls=%fused_computation.22 | loop fusion | flops 15728640 | bytes 6291456 | tf_op jit(solution)/shard_map/concatenate | solution.py:87
  100.8 12.8 %collective-permute-done.20 = bf16[384,768]{1,0:T(8,128)(2,1)S(1)} collective-permute-done((bf16[384,768]{1,0:T(8,128)(2,1)S(1)}, bf16[384,768]{1,0:T(8,128)(2,1)S(1)}, u32[]{:S(2)}, u32[]{:S(2)}) %collective-permute-start.20) | collective-permute-done | bytes 589856 | tf_op jit(solution)/shard_map/ppermute | solution.py:66
  137.7 3.1 maximum_maximum_fusion.4
  168.2 2.7 fusion.7
  187.1 16.8 %collective-permute-done.5 = bf16[280,1536]{1,0:T(8,128)(2,1)} collective-permute-done((bf16[280,1536]{1,0:T(8,128)(2,1)}, bf16[280,1536]{1,0:T(8,128)(2,1)}, u32[]{:S(2)}, u32[]{:S(2)}) %collective-permute-start.5) | collective-permute-done | bytes 860192 | tf_op jit(solution)/shard_map/ppermute | solution.py:66
  206.8 4.3 all-to-all-start
  216.7 6.7 %collective-permute-done.25 = bf16[280,1536]{1,0:T(8,128)(2,1)} collective-permute-done((bf16[280,1536]{1,0:T(8,128)(2,1)}, bf16[280,1536]{1,0:T(8,128)(2,1)}, u32[]{:S(2)}, u32[]{:S(2)}) %collective-permute-start.25) | collective-permute-done | bytes 860192 | tf_op jit(solution)/shard_map/ppermute | solution.py:66
  225.8 20.2 %all-to-all-done = bf16[128,8,192]{0,2,1:T(8,128)(2,1)} async-done(((bf16[128,8,192]{0,2,1:T(8,128)(2,1)}), bf16[128,8,192]{0,2,1:T(8,128)(2,1)}, u32[]{:S(2)}, u32[]{:S(2)}) %all-to-all-start) | async-done | bytes 393248 | tf_op jit(solution)/shard_map/all_to_all | solution.py:346
  258.1 4.1 all-to-all-start.1
  264.2 8.2 %convolution_convert_fusion = bf16[1120,1024]{1,0:T(8,128)(2,1)} fusion(bf16[1024,1536]{1,0:T(8,128)(2,1)} %all-gather.11.cloned.1.call-done, bf16[280,768]{1,0:T(8,128)(2,1)} %collective-permute-done.8, bf16[280,768]{1,0:T(8,128)(2,1)} %collective-permute-done.7, bf16[280,1536]{1,0:T(8,128)(2,1)} %collective-permute-done.6, ...), kind=kOutput, calls=%fused_computation.17 | convolution fusion | flops 3541565440 | bytes 8880128 | tf_op jit(solution)/shard_map/dot_general | solution.py:45
  272.4 4.4 all-to-all-done.1
  278.7 8.0 %fusion.78 = f32[1024,1120]{0,1:T(8,128)S(1)} fusion(bf16[1024,1536]{1,0:T(8,128)(2,1)} %all-gather.9.cloned.1.call-done, bf16[280,768]{1,0:T(8,128)(2,1)} %collective-permute-done.27, bf16[280,768]{1,0:T(8,128)(2,1)} %collective-permute-done.26, bf16[280,1536]{1,0:T(8,128)(2,1)} %collective-permute-done.25, ...), kind=kOutput, calls=%fused_computation.244 | convolution fusion | flops 3540418560 | bytes 11173888 | tf_op jit(solution)/shard_map/dot_general | solution.py:45
  286.7 9.4 %fusion.4 = (bf16[1024,1120]{0,1:T(8,128)(2,1)S(1)}, bf16[1024,1120]{0,1:T(8,128)(2,1)}, bf16[1024,1120]{0,1:T(8,128)(2,1)S(1)}) fusion(bf16[1120,1024]{1,0:T(8,128)(2,1)S(1)} %copy-done.72, f32[1024,1120]{0,1:T(8,128)S(1)} %fusion.78, bf16[1024,1536]{1,0:T(8,128)(2,1)S(1)} %copy-done.62, bf16[280,768]{1,0:T(8,128)(2,1)} %collective-permute-done.31, ...), kind=kOutput, calls=%fused_computation.11 | convolution fusion | flops 3558768640 | bytes 20348928 | tf_op jit(solution)/shard_map/dot_general | solution.py:45
  296.1 7.8 %fusion.76 = f32[1024,1536]{1,0:T(8,128)S(1)} fusion(bf16[1024,1120]{0,1:T(8,128)(2,1)S(1)} %get-tuple-element.50, bf16[280,768]{1,0:T(8,128)(2,1)} %collective-permute-done.31, bf16[280,768]{1,0:T(8,128)(2,1)} %collective-permute-done.30, bf16[280,1536]{1,0:T(8,128)(2,1)} %collective-permute-done.29, bf16[280,1536]{1,0:T(8,128)(2,1)} %collective-permute-done.28, ...), kind=kOutput, calls=%fused_computation.242 | convolution fusion | flops 3540418560 | bytes 12025856 | tf_op jit(solution)/shard_map/dot_general | solution.py:41
  304.0 7.7 %add_convert_fusion = bf16[1024,1536]{1,0:T(8,128)(2,1)} fusion(f32[1024,1536]{1,0:T(8,128)S(1)} %fusion.76, bf16[1024,1120]{0,1:T(8,128)(2,1)S(1)} %get-tuple-element.42, bf16[280,768]{1,0:T(8,128)(2,1)} %collective-permute-done.27, bf16[280,768]{1,0:T(8,128)(2,1)} %collective-permute-done.26, bf16[280,1536]{1,0:T(8,128)(2,1)} %collective-permute-done.25, ...), kind=kOutput, calls=%fused_computation.4 | convolution fusion | flops 3543564288 | bytes 15171584 | tf_op jit(solution)/shard_map/dot_general | solution.py:41
  325.1 9.3 %fusion.99 = (bf16[1120,1536]{1,0:T(8,128)(2,1)S(1)}, f32[1120,1536]{1,0:T(8,128)}) fusion(bf16[1024,1120]{0,1:T(8,128)(2,1)} %get-tuple-element.43, bf16[1024,1536]{1,0:T(8,128)(2,1)} %all-gather.11.cloned.1.call-done), kind=kOutput, calls=%fused_computation.261 | convolution fusion | flops 3524935680 | bytes 15761408 | tf_op jit(solution)/shard_map/dot_general | solution.py:51
  336.9 6.2 %fusion.97 = (bf16[1120,1536]{1,0:T(8,128)(2,1)S(1)}, f32[1120,1536]{1,0:T(8,128)}) fusion(bf16[1024,1120]{0,1:T(8,128)(2,1)S(1)} %copy-done.71, bf16[1024,1536]{1,0:T(8,128)(2,1)S(1)} %copy-done.63), kind=kOutput, calls=%fused_computation.259 | convolution fusion | flops 3524935680 | bytes 15761408 | tf_op jit(solution)/shard_map/dot_general | solution.py:51
  347.1 5.8 fusion.98
  355.4 7.7 %convolution_convert_fusion.1 = bf16[1024,1536]{1,0:T(8,128)(2,1)} fusion(bf16[1024,1120]{0,1:T(8,128)(2,1)S(1)} %copy-done.67, bf16[280,768]{1,0:T(8,128)(2,1)} %collective-permute-done.8, bf16[280,768]{1,0:T(8,128)(2,1)} %collective-permute-done.7, bf16[280,1536]{1,0:T(8,128)(2,1)} %collective-permute-done.6, ...), kind=kOutput, calls=%fused_computation.18 | convolution fusion | flops 3541991424 | bytes 8880128 | tf_op jit(solution)/shard_map/dot_general | solution.py:41
  382.0 2.6 constant_dynamic-update-slice_fusion.33
  385.3 2.8 fusion.51
  388.1 2.8 convolution_add_fusion.1
  393.7 5.7 fusion.80
  399.6 4.6 fusion.1
  407.9 2.5 copy.139
  424.9 6.5 %collective-permute-done.48 = bf16[128,1536]{1,0:T(8,128)(2,1)S(1)} collective-permute-done((bf16[128,1536]{1,0:T(8,128)(2,1)}, bf16[128,1536]{1,0:T(8,128)(2,1)S(1)}, u32[]{:S(2)}, u32[]{:S(2)}) %collective-permute-start.48) | collective-permute-done | bytes 393248 | tf_op jit(solution)/shard_map/ppermute | solution.py:66
  436.6 3.4 collective-permute-done.50
  455.5 10.4 %collective-permute-done.59 = bf16[280,1536]{1,0:T(8,128)(2,1)} collective-permute-done((bf16[280,1536]{1,0:T(8,128)(2,1)}, bf16[280,1536]{1,0:T(8,128)(2,1)}, u32[]{:S(2)}, u32[]{:S(2)}) %collective-permute-start.59) | collective-permute-done | bytes 860192 | tf_op jit(solution)/shard_map/ppermute | solution.py:66
  466.4 3.1 collective-permute-done.57
  470.7 5.4 fusion.8
  480.1 3.3 fusion.42
  483.6 4.3 collective-permute-done.53
  490.2 8.5 %collective-permute-done.37 = bf16[128,2048]{1,0:T(8,128)(2,1)} collective-permute-done((bf16[128,2048]{1,0:T(8,128)(2,1)}, bf16[128,2048]{1,0:T(8,128)(2,1)}, u32[]{:S(2)}, u32[]{:S(2)}) %collective-permute-start.37) | collective-permute-done | bytes 524320 | tf_op jit(solution)/shard_map/ppermute | solution.py:66
  501.1 3.0 convolution_add_fusion
  506.0 9.6 %maximum_maximum_fusion.5 = bf16[512,2048]{1,0:T(8,128)(2,1)S(1)} fusion(bf16[128,1024]{1,0:T(8,128)(2,1)S(1)} %collective-permute-done.40, bf16[128,1024]{1,0:T(8,128)(2,1)S(1)} %collective-permute-done.39, bf16[128,2048]{1,0:T(8,128)(2,1)} %collective-permute-done.38, bf16[128,2048]{1,0:T(8,128)(2,1)} %collective-permute-done.37, ...), kind=kLoop, calls=%fused_computation.30 | loop fusion | flops 14680064 | bytes 4194304 | tf_op jit(solution)/shard_map/concatenate | solution.py:87
  515.7 3.5 fusion.12
  522.9 2.7 constant_dynamic-update-slice_fusion.29
  525.5 3.6 convolution_convert_fusion.2
  534.5 3.2 constant_dynamic-update-slice_fusion.16
  537.7 4.2 convolution_convert_fusion.3
  547.6 2.8 collective-permute-done.45
  557.9 16.1 %reduce-scatter.9.cloned.1.call-done = bf16[48,2048]{1,0:T(8,128)(2,1)} async-done(((bf16[192,2048]{1,0:T(8,128)(2,1)}), bf16[48,2048]{1,0:T(8,128)(2,1)}) %reduce-scatter.9.cloned.1.call-update) | async-done | bytes 196624 | tf_op jit(solution)/shard_map/reduce_scatter | solution.py:355
  (459 shorter events, 260.9 us)
Async XLA Ops:
  7.2 32.6 %all-gather.5.cloned.1.call-start = ((), (), s32[]{:S(2)}) async-start(), calls=%async_computation.6 | async-start | bytes 1769472 | tf_op jit(solution)/shard_map/all_gather | solution.py:160
  10.3 86.3 %all-gather.7.cloned.1.call-start = ((), (), s32[]{:S(2)}) async-start(), calls=%async_computation.7 | async-start | bytes 1327104 | tf_op jit(solution)/shard_map/all_gather | solution.py:160
  41.0 19.7 %collective-permute-start.10 = (bf16[384,1024]{1,0:T(8,128)(2,1)S(1)}, bf16[384,1024]{1,0:T(8,128)(2,1)S(1)}, u32[]{:S(2)}, u32[]{:S(2)}) collective-permute-start(bf16[384,1024]{1,0:T(8,128)(2,1)S(1)} %constant_dynamic-slice_fusion.11), channel_id=1, source_target_pairs={{0,16},{8,24},{16,0},{24,8},{1,17},{9,25},{17,1},{25,9},{2,18},{10... | collective-permute-start | bytes 2359304 | tf_op jit(solution)/shard_map/ppermute | solution.py:66
  42.6 19.8 %collective-permute-start.9 = (bf16[384,1024]{1,0:T(8,128)(2,1)S(1)}, bf16[384,1024]{1,0:T(8,128)(2,1)S(1)}, u32[]{:S(2)}, u32[]{:S(2)}) collective-permute-start(bf16[384,1024]{1,0:T(8,128)(2,1)S(1)} %constant_dynamic-slice_fusion.11), channel_id=1, source_target_pairs={{0,8},{8,0},{16,24},{24,16},{1,9},{9,1},{17,25},{25,17},{2,10},{10... | collective-permute-start | bytes 2359304 | tf_op jit(solution)/shard_map/ppermute | solution.py:66
  44.1 220.1 %all-gather.11.cloned.1.call-start = ((), (), s32[]{:S(2)}) async-start(), calls=%async_computation.10 | async-start | bytes 3538944 | tf_op jit(solution)/shard_map/all_gather | solution.py:229
  81.9 35.4 %collective-permute-start.13 = (bf16[1536,1024]{1,0:T(8,128)(2,1)S(1)}, bf16[1536,1024]{1,0:T(8,128)(2,1)}, u32[]{:S(2)}, u32[]{:S(2)}) collective-permute-start(bf16[1536,1024]{1,0:T(8,128)(2,1)S(1)} %maximum_maximum_fusion.3), channel_id=1, source_target_pairs={{0,4},{4,0},{1,5},{5,1},{2,6},{6,2},{3,7},{7,3},{8,12},{12,8},{9,1... | collective-permute-start | bytes 9437192 | tf_op jit(solution)/shard_map/ppermute | solution.py:70
  82.0 196.6 %all-gather.9.cloned.1.call-start = ((), (), s32[]{:S(2)}) async-start(), calls=%async_computation.8 | async-start | bytes 3538944 | tf_op jit(solution)/shard_map/all_gather | solution.py:275
  97.8 15.8 %collective-permute-start.20 = (bf16[384,768]{1,0:T(8,128)(2,1)S(1)}, bf16[384,768]{1,0:T(8,128)(2,1)S(1)}, u32[]{:S(2)}, u32[]{:S(2)}) collective-permute-start(bf16[384,768]{1,0:T(8,128)(2,1)S(1)} %constant_dynamic-slice_fusion.5), channel_id=1, source_target_pairs={{0,16},{8,24},{16,0},{24,8},{1,17},{9,25},{17,1},{25,9},{2,18},{10... | collective-permute-start | bytes 1769480 | tf_op jit(solution)/shard_map/ppermute | solution.py:66
  99.3 16.1 %collective-permute-start.19 = (bf16[384,768]{1,0:T(8,128)(2,1)S(1)}, bf16[384,768]{1,0:T(8,128)(2,1)S(1)}, u32[]{:S(2)}, u32[]{:S(2)}) collective-permute-start(bf16[384,768]{1,0:T(8,128)(2,1)S(1)} %constant_dynamic-slice_fusion.5), channel_id=1, source_target_pairs={{0,8},{8,0},{16,24},{24,16},{1,9},{9,1},{17,25},{25,17},{2,10},{10... | collective-permute-start | bytes 1769480 | tf_op jit(solution)/shard_map/ppermute | solution.py:66
  114.4 23.2 %collective-permute-start.22 = (bf16[384,384]{1,0:T(8,128)(2,1)}, bf16[384,384]{1,0:T(8,128)(2,1)}, u32[]{:S(2)}, u32[]{:S(2)}) collective-permute-start(bf16[384,384]{1,0:T(8,128)(2,1)} %slice.436), channel_id=1, source_target_pairs={{0,8},{8,0},{16,24},{24,16},{1,9},{9,1},{17,25},{25,17},{2,10},{10... | collective-permute-start | bytes 884744 | tf_op jit(solution)/shard_map/ppermute | solution.py:66
  116.3 21.4 %collective-permute-start.21 = (bf16[384,384]{1,0:T(8,128)(2,1)}, bf16[384,384]{1,0:T(8,128)(2,1)}, u32[]{:S(2)}, u32[]{:S(2)}) collective-permute-start(bf16[384,384]{1,0:T(8,128)(2,1)} %slice.435), channel_id=1, source_target_pairs={{0,16},{8,24},{16,0},{24,8},{1,17},{9,25},{17,1},{25,9},{2,18},{10... | collective-permute-start | bytes 884744 | tf_op jit(solution)/shard_map/ppermute | solution.py:66
  140.8 34.1 %collective-permute-start.23 = (bf16[1536,768]{1,0:T(8,128)(2,1)}, bf16[1536,768]{1,0:T(8,128)(2,1)}, u32[]{:S(2)}, u32[]{:S(2)}) collective-permute-start(bf16[1536,768]{1,0:T(8,128)(2,1)} %maximum_maximum_fusion.4), channel_id=1, source_target_pairs={{0,4},{4,0},{1,5},{5,1},{2,6},{6,2},{3,7},{7,3},{8,12},{12,8},{9,1... | collective-permute-start | bytes 7077896 | tf_op jit(solution)/shard_map/ppermute | solution.py:70
  181.5 22.4 %collective-permute-start.5 = (bf16[280,1536]{1,0:T(8,128)(2,1)}, bf16[280,1536]{1,0:T(8,128)(2,1)}, u32[]{:S(2)}, u32[]{:S(2)}) collective-permute-start(bf16[280,1536]{1,0:T(8,128)(2,1)} %param.28), channel_id=1, source_target_pairs={{0,8},{8,0},{16,24},{24,16},{1,9},{9,1},{17,25},{25,17},{2,10},{10... | collective-permute-start | bytes 2580488 | tf_op jit(solution)/shard_map/ppermute | solution.py:66
  182.6 30.3 %collective-permute-start.6 = (bf16[280,1536]{1,0:T(8,128)(2,1)}, bf16[280,1536]{1,0:T(8,128)(2,1)}, u32[]{:S(2)}, u32[]{:S(2)}) collective-permute-start(bf16[280,1536]{1,0:T(8,128)(2,1)} %param.28), channel_id=1, source_target_pairs={{0,16},{8,24},{16,0},{24,8},{1,17},{9,25},{17,1},{25,9},{2,18},{10... | collective-permute-start | bytes 2580488 | tf_op jit(solution)/shard_map/ppermute | solution.py:66
  183.6 39.8 %collective-permute-start.25 = (bf16[280,1536]{1,0:T(8,128)(2,1)}, bf16[280,1536]{1,0:T(8,128)(2,1)}, u32[]{:S(2)}, u32[]{:S(2)}) collective-permute-start(bf16[280,1536]{1,0:T(8,128)(2,1)} %bitcast.170), channel_id=1, source_target_pairs={{0,16},{8,24},{16,0},{24,8},{1,17},{9,25},{17,1},{25,9},{2,18},{10... | collective-permute-start | bytes 2580488 | tf_op jit(solution)/shard_map/ppermute | solution.py:66
  184.6 65.0 %collective-permute-start.24 = (bf16[280,1536]{1,0:T(8,128)(2,1)}, bf16[280,1536]{1,0:T(8,128)(2,1)}, u32[]{:S(2)}, u32[]{:S(2)}) collective-permute-start(bf16[280,1536]{1,0:T(8,128)(2,1)} %bitcast.171), channel_id=1, source_target_pairs={{0,8},{8,0},{16,24},{24,16},{1,9},{9,1},{17,25},{25,17},{2,10},{10... | collective-permute-start | bytes 2580488 | tf_op jit(solution)/shard_map/ppermute | solution.py:66
  185.6 66.8 %collective-permute-start.29 = (bf16[280,1536]{1,0:T(8,128)(2,1)}, bf16[280,1536]{1,0:T(8,128)(2,1)}, u32[]{:S(2)}, u32[]{:S(2)}) collective-permute-start(bf16[280,1536]{1,0:T(8,128)(2,1)} %bitcast.166), channel_id=1, source_target_pairs={{0,16},{8,24},{16,0},{24,8},{1,17},{9,25},{17,1},{25,9},{2,18},{10... | collective-permute-start | bytes 2580488 | tf_op jit(solution)/shard_map/ppermute | solution.py:66
  203.8 51.9 %collective-permute-start.28 = (bf16[280,1536]{1,0:T(8,128)(2,1)}, bf16[280,1536]{1,0:T(8,128)(2,1)}, u32[]{:S(2)}, u32[]{:S(2)}) collective-permute-start(bf16[280,1536]{1,0:T(8,128)(2,1)} %bitcast.167), channel_id=1, source_target_pairs={{0,8},{8,0},{16,24},{24,16},{1,9},{9,1},{17,25},{25,17},{2,10},{10... | collective-permute-start | bytes 2580488 | tf_op jit(solution)/shard_map/ppermute | solution.py:66
  206.8 39.2 %all-to-all-start = ((bf16[128,8,192]{0,2,1:T(8,128)(2,1)}), bf16[128,8,192]{0,2,1:T(8,128)(2,1)}, u32[]{:S(2)}, u32[]{:S(2)}) async-start(bf16[128,8,192]{0,2,1:T(8,128)(2,1)} %bitcast.143), calls=%async_computation.2 | async-start | bytes 786432 | tf_op jit(solution)/shard_map/all_to_all | solution.py:346
  212.9 49.3 %collective-permute-start.7 = (bf16[280,768]{1,0:T(8,128)(2,1)}, bf16[280,768]{1,0:T(8,128)(2,1)}, u32[]{:S(2)}, u32[]{:S(2)}) collective-permute-start(bf16[280,768]{1,0:T(8,128)(2,1)} %slice.417), channel_id=1, source_target_pairs={{0,16},{8,24},{16,0},{24,8},{1,17},{9,25},{17,1},{25,9},{2,18},{10... | collective-permute-start | bytes 1290248 | tf_op jit(solution)/shard_map/ppermute | solution.py:66
  223.4 40.8 %collective-permute-start.8 = (bf16[280,768]{1,0:T(8,128)(2,1)}, bf16[280,768]{1,0:T(8,128)(2,1)}, u32[]{:S(2)}, u32[]{:S(2)}) collective-permute-start(bf16[280,768]{1,0:T(8,128)(2,1)} %slice.418), channel_id=1, source_target_pairs={{0,8},{8,0},{16,24},{24,16},{1,9},{9,1},{17,25},{25,17},{2,10},{10... | collective-permute-start | bytes 1290248 | tf_op jit(solution)/shard_map/ppermute | solution.py:66
  249.7 29.0 %collective-permute-start.27 = (bf16[280,768]{1,0:T(8,128)(2,1)}, bf16[280,768]{1,0:T(8,128)(2,1)}, u32[]{:S(2)}, u32[]{:S(2)}) collective-permute-start(bf16[280,768]{1,0:T(8,128)(2,1)} %slice.439), channel_id=1, source_target_pairs={{0,8},{8,0},{16,24},{24,16},{1,9},{9,1},{17,25},{25,17},{2,10},{10... | collective-permute-start | bytes 1290248 | tf_op jit(solution)/shard_map/ppermute | solution.py:66
  252.4 26.2 %collective-permute-start.26 = (bf16[280,768]{1,0:T(8,128)(2,1)}, bf16[280,768]{1,0:T(8,128)(2,1)}, u32[]{:S(2)}, u32[]{:S(2)}) collective-permute-start(bf16[280,768]{1,0:T(8,128)(2,1)} %slice.438), channel_id=1, source_target_pairs={{0,16},{8,24},{16,0},{24,8},{1,17},{9,25},{17,1},{25,9},{2,18},{10... | collective-permute-start | bytes 1290248 | tf_op jit(solution)/shard_map/ppermute | solution.py:66
  255.7 30.9 %collective-permute-start.31 = (bf16[280,768]{1,0:T(8,128)(2,1)}, bf16[280,768]{1,0:T(8,128)(2,1)}, u32[]{:S(2)}, u32[]{:S(2)}) collective-permute-start(bf16[280,768]{1,0:T(8,128)(2,1)} %slice.441), channel_id=1, source_target_pairs={{0,8},{8,0},{16,24},{24,16},{1,9},{9,1},{17,25},{25,17},{2,10},{10... | collective-permute-start | bytes 1290248 | tf_op jit(solution)/shard_map/ppermute | solution.py:66
  258.1 18.7 %all-to-all-start.1 = ((bf16[128,8,192]{0,2,1:T(8,128)(2,1)}), bf16[128,8,192]{0,2,1:T(8,128)(2,1)}, u32[]{:S(2)}, u32[]{:S(2)}) async-start(bf16[128,8,192]{0,2,1:T(8,128)(2,1)} %bitcast.142), calls=%async_computation.4 | async-start | bytes 786432 | tf_op jit(solution)/shard_map/all_to_all | solution.py:346
  262.2 118.2 %reduce-scatter.7.cloned.1.call-start = ((), (), s32[]{:S(2)}) async-start(), calls=%async_computation.11 | async-start | bytes 3538944 | tf_op jit(solution)/shard_map/reduce_scatter | solution.py:285
  262.3 24.4 %collective-permute-start.30 = (bf16[280,768]{1,0:T(8,128)(2,1)}, bf16[280,768]{1,0:T(8,128)(2,1)}, u32[]{:S(2)}, u32[]{:S(2)}) collective-permute-start(bf16[280,768]{1,0:T(8,128)(2,1)} %slice.440), channel_id=1, source_target_pairs={{0,16},{8,24},{16,0},{24,8},{1,17},{9,25},{17,1},{25,9},{2,18},{10... | collective-permute-start | bytes 1290248 | tf_op jit(solution)/shard_map/ppermute | solution.py:66
  311.7 235.8 %reduce-scatter.5.cloned.1.call-start = ((), (), s32[]{:S(2)}) async-start(), calls=%async_computation.9 | async-start | bytes 3538944 | tf_op jit(solution)/shard_map/reduce_scatter | solution.py:289
  335.6 28.0 %collective-permute-start.62 = (bf16[280,768]{1,0:T(8,128)(2,1)}, bf16[280,768]{1,0:T(8,128)(2,1)}, u32[]{:S(2)}, u32[]{:S(2)}) collective-permute-start(bf16[280,768]{1,0:T(8,128)(2,1)} %get-tuple-element.53), channel_id=1, source_target_pairs={{0,8},{8,0},{16,24},{24,16},{1,9},{9,1},{17,25},{25,17},{2,10},{10... | collective-permute-start | bytes 1290248 | tf_op jit(solution)/shard_map/ppermute | solution.py:66
  335.7 28.5 %collective-permute-start.60 = (bf16[280,768]{1,0:T(8,128)(2,1)}, bf16[280,768]{1,0:T(8,128)(2,1)}, u32[]{:S(2)}, u32[]{:S(2)}) collective-permute-start(bf16[280,768]{1,0:T(8,128)(2,1)} %get-tuple-element.54), channel_id=1, source_target_pairs={{0,16},{8,24},{16,0},{24,8},{1,17},{9,25},{17,1},{25,9},{2,18},{10... | collective-permute-start | bytes 1290248 | tf_op jit(solution)/shard_map/ppermute | solution.py:66
  344.3 25.2 %collective-permute-start.54 = (bf16[280,768]{1,0:T(8,128)(2,1)}, bf16[280,768]{1,0:T(8,128)(2,1)}, u32[]{:S(2)}, u32[]{:S(2)}) collective-permute-start(bf16[280,768]{1,0:T(8,128)(2,1)} %get-tuple-element.61), channel_id=1, source_target_pairs={{0,8},{8,0},{16,24},{24,16},{1,9},{9,1},{17,25},{25,17},{2,10},{10... | collective-permute-start | bytes 1290248 | tf_op jit(solution)/shard_map/ppermute | solution.py:66
  345.6 24.6 %collective-permute-start.52 = (bf16[280,768]{1,0:T(8,128)(2,1)}, bf16[280,768]{1,0:T(8,128)(2,1)}, u32[]{:S(2)}, u32[]{:S(2)}) collective-permute-start(bf16[280,768]{1,0:T(8,128)(2,1)} %get-tuple-element.62), channel_id=1, source_target_pairs={{0,16},{8,24},{16,0},{24,8},{1,17},{9,25},{17,1},{25,9},{2,18},{10... | collective-permute-start | bytes 1290248 | tf_op jit(solution)/shard_map/ppermute | solution.py:66
  354.1 20.5 %collective-permute-start.58 = (bf16[280,768]{1,0:T(8,128)(2,1)}, bf16[280,768]{1,0:T(8,128)(2,1)}, u32[]{:S(2)}, u32[]{:S(2)}) collective-permute-start(bf16[280,768]{1,0:T(8,128)(2,1)} %get-tuple-element.57), channel_id=1, source_target_pairs={{0,8},{8,0},{16,24},{24,16},{1,9},{9,1},{17,25},{25,17},{2,10},{10... | collective-permute-start | bytes 1290248 | tf_op jit(solution)/shard_map/ppermute | solution.py:66
  363.0 193.2 %reduce-scatter.11.cloned.1.call-start = ((), (), s32[]{:S(2)}) async-start(), calls=%async_computation.13 | async-start | bytes 737280 | tf_op jit(solution)/shard_map/reduce_scatter | solution.py:349
  367.0 87.6 %collective-permute-start.63 = (bf16[280,1536]{1,0:T(8,128)(2,1)}, bf16[280,1536]{1,0:T(8,128)(2,1)}, u32[]{:S(2)}, u32[]{:S(2)}) collective-permute-start(bf16[280,1536]{1,0:T(8,128)(2,1)} %pad_maximum_fusion.6), channel_id=1, source_target_pairs={{0,16},{8,24},{16,0},{24,8},{1,17},{9,25},{17,1},{25,9},{2,18},{10... | collective-permute-start | bytes 2580488 | tf_op jit(solution)/shard_map/ppermute | solution.py:66
  369.5 86.0 %collective-permute-start.61 = (bf16[280,1536]{1,0:T(8,128)(2,1)}, bf16[280,1536]{1,0:T(8,128)(2,1)}, u32[]{:S(2)}, u32[]{:S(2)}) collective-permute-start(bf16[280,1536]{1,0:T(8,128)(2,1)} %pad_maximum_fusion.5), channel_id=1, source_target_pairs={{0,8},{8,0},{16,24},{24,16},{1,9},{9,1},{17,25},{25,17},{2,10},{10... | collective-permute-start | bytes 2580488 | tf_op jit(solution)/shard_map/ppermute | solution.py:66
  373.0 110.6 %collective-permute-start.55 = (bf16[280,1536]{1,0:T(8,128)(2,1)}, bf16[280,1536]{1,0:T(8,128)(2,1)}, u32[]{:S(2)}, u32[]{:S(2)}) collective-permute-start(bf16[280,1536]{1,0:T(8,128)(2,1)} %pad_maximum_fusion.2), channel_id=1, source_target_pairs={{0,16},{8,24},{16,0},{24,8},{1,17},{9,25},{17,1},{25,9},{2,18},{10... | collective-permute-start | bytes 2580488 | tf_op jit(solution)/shard_map/ppermute | solution.py:66
  384.6 35.0 %collective-permute-start.47 = (bf16[128,1536]{1,0:T(8,128)(2,1)}, bf16[128,1536]{1,0:T(8,128)(2,1)}, u32[]{:S(2)}, u32[]{:S(2)}) collective-permute-start(bf16[128,1536]{1,0:T(8,128)(2,1)} %get-tuple-element.33), channel_id=1, source_target_pairs={{0,8},{8,0},{16,24},{24,16},{1,9},{9,1},{17,25},{25,17},{2,10},{10... | collective-permute-start | bytes 1179656 | tf_op jit(solution)/shard_map/ppermute | solution.py:66
  446.6 19.3 %collective-permute-start.59 = (bf16[280,1536]{1,0:T(8,128)(2,1)}, bf16[280,1536]{1,0:T(8,128)(2,1)}, u32[]{:S(2)}, u32[]{:S(2)}) collective-permute-start(bf16[280,1536]{1,0:T(8,128)(2,1)} %pad_maximum_fusion.4), channel_id=1, source_target_pairs={{0,16},{8,24},{16,0},{24,8},{1,17},{9,25},{17,1},{25,9},{2,18},{10... | collective-permute-start | bytes 2580488 | tf_op jit(solution)/shard_map/ppermute | solution.py:66
  447.1 22.4 %collective-permute-start.57 = (bf16[280,1536]{1,0:T(8,128)(2,1)}, bf16[280,1536]{1,0:T(8,128)(2,1)}, u32[]{:S(2)}, u32[]{:S(2)}) collective-permute-start(bf16[280,1536]{1,0:T(8,128)(2,1)} %pad_maximum_fusion.3), channel_id=1, source_target_pairs={{0,8},{8,0},{16,24},{24,16},{1,9},{9,1},{17,25},{25,17},{2,10},{10... | collective-permute-start | bytes 2580488 | tf_op jit(solution)/shard_map/ppermute | solution.py:66
  454.6 33.3 %collective-permute-start.53 = (bf16[280,1536]{1,0:T(8,128)(2,1)}, bf16[280,1536]{1,0:T(8,128)(2,1)}, u32[]{:S(2)}, u32[]{:S(2)}) collective-permute-start(bf16[280,1536]{1,0:T(8,128)(2,1)} %pad_maximum_fusion.1), channel_id=1, source_target_pairs={{0,8},{8,0},{16,24},{24,16},{1,9},{9,1},{17,25},{25,17},{2,10},{10... | collective-permute-start | bytes 2580488 | tf_op jit(solution)/shard_map/ppermute | solution.py:66
  455.5 67.4 %collective-permute-start.51 = (bf16[512,1536]{1,0:T(8,128)(2,1)}, bf16[512,1536]{1,0:T(8,128)(2,1)}, u32[]{:S(2)}, u32[]{:S(2)}) collective-permute-start(bf16[512,1536]{1,0:T(8,128)(2,1)} %maximum_maximum_fusion.6), channel_id=1, source_target_pairs={{0,4},{4,0},{1,5},{5,1},{2,6},{6,2},{3,7},{7,3},{8,12},{12,8},{9,1... | collective-permute-start | bytes 4718600 | tf_op jit(solution)/shard_map/ppermute | solution.py:70
  465.9 22.0 %collective-permute-start.38 = (bf16[128,2048]{1,0:T(8,128)(2,1)}, bf16[128,2048]{1,0:T(8,128)(2,1)}, u32[]{:S(2)}, u32[]{:S(2)}) collective-permute-start(bf16[128,2048]{1,0:T(8,128)(2,1)} %get-tuple-element.35), channel_id=1, source_target_pairs={{0,16},{8,24},{16,0},{24,8},{1,17},{9,25},{17,1},{25,9},{2,18},{10... | collective-permute-start | bytes 1572872 | tf_op jit(solution)/shard_map/ppermute | solution.py:66
  469.5 29.1 %collective-permute-start.37 = (bf16[128,2048]{1,0:T(8,128)(2,1)}, bf16[128,2048]{1,0:T(8,128)(2,1)}, u32[]{:S(2)}, u32[]{:S(2)}) collective-permute-start(bf16[128,2048]{1,0:T(8,128)(2,1)} %get-tuple-element.35), channel_id=1, source_target_pairs={{0,8},{8,0},{16,24},{24,16},{1,9},{9,1},{17,25},{25,17},{2,10},{10... | collective-permute-start | bytes 1572872 | tf_op jit(solution)/shard_map/ppermute | solution.py:66
  483.6 37.5 %collective-permute-start.42 = (f32[32,112]{1,0:T(8,128)S(1)}, f32[32,112]{1,0:T(8,128)S(1)}, u32[]{:S(2)}, u32[]{:S(2)}) collective-permute-start(f32[32,112]{1,0:T(8,128)S(1)} %pad_maximum_fusion.24), channel_id=1, source_target_pairs={{0,4},{4,0},{1,5},{5,1},{2,6},{6,2},{3,7},{7,3},{8,12},{12,8},{9,1... | collective-permute-start | bytes 43016 | tf_op jit(solution)/shard_map/ppermute | solution.py:171
  515.6 18.9 %collective-permute-start.41 = (bf16[512,2048]{1,0:T(8,128)(2,1)S(1)}, bf16[512,2048]{1,0:T(8,128)(2,1)}, u32[]{:S(2)}, u32[]{:S(2)}) collective-permute-start(bf16[512,2048]{1,0:T(8,128)(2,1)S(1)} %maximum_maximum_fusion.5), channel_id=1, source_target_pairs={{0,4},{4,0},{1,5},{5,1},{2,6},{6,2},{3,7},{7,3},{8,12},{12,8},{9,1... | collective-permute-start | bytes 6291464 | tf_op jit(solution)/shard_map/ppermute | solution.py:70
  521.7 20.4 %collective-permute-start.43 = (f32[32,112]{1,0:T(8,128)}, f32[32,112]{1,0:T(8,128)}, u32[]{:S(2)}, u32[]{:S(2)}) collective-permute-start(f32[32,112]{1,0:T(8,128)} %add.286), channel_id=1, source_target_pairs={{0,8},{8,0},{16,24},{24,16},{1,9},{9,1},{17,25},{25,17},{2,10},{10... | collective-permute-start | bytes 43016 | tf_op jit(solution)/shard_map/ppermute | solution.py:171
  529.1 44.8 %reduce-scatter.9.cloned.1.call-start = ((), (), s32[]{:S(2)}) async-start(), calls=%async_computation.12 | async-start | bytes 983040 | tf_op jit(solution)/shard_map/reduce_scatter | solution.py:355
  (99 other events, 795.5 us)
Sparse Core Ops, SparseCore 0:
  10.5 29.3 all-gather.4
  44.2 20.1 all-gather.6
  82.1 36.9 all-gather.10
  181.6 36.7 all-gather.8
  311.9 37.8 reduce-scatter.6
  363.2 38.0 reduce-scatter.4
  529.2 20.6 reduce-scatter.10
  552.2 21.6 reduce-scatter.8
